TPU v7x, 128 devices: a whole 4x4x4 slice. The times are simulated.
128 devices in a mesh: grp: 8 (over x, y_hi), blk: 16 (over y_lo, z, core).
Axes of the slice: x: 4, y: 4 (y_hi: 2, y_lo: 2; y = y_hi * 2 + y_lo), z: 4, core: 2. Of those that a mesh axis runs over, the one named last changes fastest.
Arguments:
- integrals: float32 [96, 1024, 1536], P('grp', 'blk'), may hold values from -0.9 to 0.9
- pair_lists: int32 [8, 2], P('grp'), may hold values from 0 to 96, as said below
- row_orbital: int32 [96], P('grp'), may hold values from 0 to 95, each once
- occ_energy: float32 [96], replicated, may hold values from -2 to -0.5
- vir_energy: float32 [1024], P('blk'), may hold values from 0.5 to 4
Outputs:
- three_index_density: float32 [96, 1024, 1536], P('grp', 'blk')
Inputs may be any that keep to these rules, and one draw needn't show every extreme that they name: `pair_lists`: entries are rows of the integrals, or 96 in unused slots; used slots come first; every group lists one to 2 rows, some group exactly one and some exactly 2; no two rows listed by one group are held by the same group (a group may list one of its own rows). `row_orbital`: each orbital stands in exactly one row.
All inputs are finite; a program needn't handle non-finite values.
Results may differ from a plain program's by a relative error of at most 0.0001.
Values sent between devices are 32-bit elements; how exact they have to be, the bound alone decides.
A program may use at most 128 MiB of HBM per device.

v0:
```python
import jax
import jax.numpy as jnp
from jax import lax
from jax.sharding import PartitionSpec as P


def body(integrals, pair_lists, row_orbital, occ_energy, vir_energy):
    highest = lax.Precision.HIGHEST
    own_count, vir_width, aux_width = integrals.shape
    slot_count = pair_lists.shape[1]
    group_count = lax.axis_size("grp")
    group_place = lax.axis_index("grp")
    listed, orbitals = (
        lax.all_gather(pair_lists, "grp", axis=0, tiled=True),
        lax.all_gather(row_orbital, "grp", axis=0, tiled=True),
    )
    total_rows = orbitals.shape[0]
    columns = lax.broadcasted_iota(jnp.int32, (group_count, slot_count, total_rows), 2)
    matches = (listed[:, :, None] == columns).astype(jnp.float32)
    held_rows = lax.dynamic_slice_in_dim(matches, group_place * own_count, own_count, 2)
    selected = jnp.sum(held_rows, axis=1)
    outgoing = jnp.einsum("gr,rap->gap", selected, integrals, precision=highest)
    incoming = lax.all_to_all(outgoing, "grp", split_axis=0, concat_axis=0, tiled=True)
    own_match = lax.dynamic_index_in_dim(matches, group_place, 0, keepdims=False)
    owner_pick = jnp.sum(own_match.reshape(slot_count, group_count, own_count), axis=2)
    partner = jnp.einsum("js,sap->jap", owner_pick, incoming, precision=highest)
    orbital_ids = lax.broadcasted_iota(jnp.int32, (total_rows, occ_energy.shape[0]), 1)
    lookup = (orbitals[:, None] == orbital_ids).astype(jnp.float32)
    row_energy = jnp.dot(lookup, occ_energy, precision=highest)
    own_energy = lax.dynamic_slice_in_dim(row_energy, group_place * own_count, own_count, 0)
    partner_energy = jnp.dot(own_match, row_energy, precision=highest)
    vir_rows = vir_energy.reshape(1, vir_width)
    blocks = lax.all_gather(partner, "blk", axis=1, tiled=True)
    energies = lax.all_gather(vir_rows, "blk", axis=1, tiled=True)
    pair_block = jnp.einsum("iap,jbp->iajb", integrals, blocks, precision=highest)
    denominator = (
        own_energy[:, None, None, None]
        + partner_energy[None, None, :, None]
        - vir_energy[None, :, None, None]
        - energies[0][None, None, None, :]
    )
    amplitude = pair_block / denominator
    density_own = jnp.einsum("iajb,jbp->iap", amplitude, blocks, precision=highest)
    amplitudes = amplitude
    density_own, amplitudes = (density_own, amplitudes)
    density_term = jnp.einsum("iajb,iap->bjp", amplitudes, integrals, precision=highest)
    summed = lax.psum(density_term, "blk")
    own_share = lax.dynamic_slice_in_dim(summed, lax.axis_index("blk") * vir_width, vir_width, 0)
    returning = jnp.einsum("bjp,js->bsp", own_share, owner_pick, precision=highest)
    arrived = lax.all_to_all(returning, "grp", split_axis=1, concat_axis=1, tiled=True)
    return density_own + jnp.einsum("sr,bsp->rbp", selected, arrived, precision=highest)


def solution(mesh):
    in_specs = (P("grp", "blk", None), P("grp", None), P("grp"), P(), P("blk"))
    out_specs = P("grp", "blk", None)
    return jax.shard_map(body, mesh=mesh, in_specs=in_specs, out_specs=out_specs, check_vma=False)
```

profile of v0, /device:TPU:0, one launch (start us, length us, event | category | flops | bytes accessed | tf_op | source)
XLA Modules:
  0.0 500.9 jit_solution(10788057411563792185)
XLA Ops:
  6.5 23.9 %all-gather.1 = s32[8,1,2]{2,1,0:T(1,128)S(1)} all-gather(s32[1,1,2]{2,1,0:T(1,128)} %bitcast.51), channel_id=1, replica_groups=mesh['grp'=8,'blk'=16] {'grp'}, dimensions={0}, use_global_device_ids=true | all-gather | bytes 72 | tf_op jit(solution)/shard_map/all_gather | solution.py:14
  30.4 0.1 iota_compare_fusion.2
  30.5 0.1 dynamic-slice_reduce_fusion
  30.6 8.8 %fusion.6 = f32[8,64,1536]{2,0,1:T(8,128)S(1)} fusion(f32[12,64,1536]{2,1,0:T(8,128)} %param.5, f32[8,12]{1,0:T(8,128)S(1)} %dynamic-slice_reduce_fusion), kind=kOutput, calls=%fused_computation.8 | convolution fusion | flops 113246208 | bytes 7864704 | tf_op jit(solution)/shard_map/gr,rap->gap/dot_general | solution.py:22
  39.4 3.5 copy.34
  42.9 3.8 all-to-all-start
  46.7 0.1 reshape.48
  46.8 0.1 reduce_sum.18
  46.9 40.4 %all-to-all-done = f32[8,64,1536]{2,1,0:T(8,128)S(1)} async-done(((f32[8,64,1536]{2,1,0:T(8,128)}), f32[8,64,1536]{2,1,0:T(8,128)S(1)}, u32[]{:S(2)}, u32[]{:S(2)}) %all-to-all-start) | async-done | bytes 3145760 | tf_op jit(solution)/shard_map/all_to_all | solution.py:23
  87.3 5.2 %fusion.14 = f32[2,64,1536]{2,0,1:T(2,128)} fusion(f32[8,64,1536]{2,1,0:T(8,128)S(1)} %all-to-all-done, f32[2,8]{1,0:T(2,128)S(1)} %reduce_sum.18), kind=kOutput, calls=%fused_computation.16 | convolution fusion | flops 18874368 | bytes 3932224 | tf_op jit(solution)/shard_map/js,sap->jap/dot_general | solution.py:26
  92.6 0.6 dynamic-slice.1
  93.2 0.6 dynamic-slice
  94.5 0.2 dynamic-update-slice
  94.7 9.6 %all-reduce = s32[96]{0:T(128)S(1)} all-reduce(s32[96]{0:T(128)S(1)} %dynamic-update-slice), channel_id=1, replica_groups=mesh['grp'=8,'blk'=16] {'grp'}, use_global_device_ids=true, to_apply=%add | all-reduce | flops 96 | bytes 768
  104.3 0.2 fusion.21
  104.5 0.1 dynamic_slice.17
  105.3 0.2 dynamic-update-slice.1
  105.5 29.0 %all-reduce.1 = f32[1024]{0:T(1024)S(1)} all-reduce(f32[1024]{0:T(1024)S(1)} %dynamic-update-slice.1), channel_id=2, replica_groups=mesh['grp'=8,'blk'=16] {'blk'}, use_global_device_ids=true, to_apply=%add.1 | all-reduce | flops 1024 | bytes 8192
  134.6 0.1 convolution_bitcast_fusion.2
  134.7 0.1 broadcast_add_fusion
  134.8 0.1 broadcast_subtract_fusion
  134.8 27.4 %all-gather.4.cloned.1.call-done = f32[2,1024,1536]{2,0,1:T(2,128)} async-done(((f32[2,64,1536]{2,0,1:T(2,128)}), f32[2,1024,1536]{2,0,1:T(2,128)}) %all-gather.4.cloned.1.call-update) | async-done | bytes 12582928 | tf_op jit(solution)/shard_map/all_gather | solution.py:33
  162.2 37.8 %fusion.2 = f32[2,1024,12,64]{1,3,2,0:T(8,128)S(1)} fusion(f32[2,1024,1536,1]{2,0,1,3:T(2,128)} %bitcast.53, f32[12,64,1536]{2,1,0:T(8,128)} %param.5), kind=kOutput, calls=%fused_computation.2 | convolution fusion | flops 28991029248 | bytes 23592960 | tf_op jit(solution)/shard_map/iap,jbp->iajb/dot_general | solution.py:35
  200.1 2.6 copy-done.6
  202.7 35.0 %convolution_bitcast_fusion = f32[1024,2,1536]{2,0,1:T(8,128)} fusion(f32[2,1024,12,64]{1,3,2,0:T(8,128)S(1)} %fusion.2, f32[12,64,1536]{2,1,0:T(8,128)S(1)} %bitcast.49, f32[1024]{0:T(1024)S(1)} %all-reduce.1, f32[12,64,2]{1,0,2:T(8,128)S(1)} %broadcast_subtract_fusion), kind=kOutput, calls=%fused_computation.4 | convolution fusion | flops 28994174976 | bytes 23603200 | tf_op jit(solution)/shard_map/iajb,iap->bjp/dot_general | solution.py:46
  237.7 160.2 %all-reduce.4.cloned.1.call-done = f32[1024,2,1536]{2,0,1:T(8,128)} async-done(((f32[1024,2,1536]{2,0,1:T(8,128)}), f32[1024,2,1536]{2,0,1:T(8,128)}) %all-reduce.4.cloned.1.call-update) | async-done | bytes 12582928 | tf_op jit(solution)/shard_map/psum | solution.py:47
  397.9 1.2 constant_dynamic-slice_fusion
  399.1 3.8 convolution_bitcast_fusion.1
  402.9 1.8 copy.39
  404.8 44.4 %all_to_all.10 = f32[64,8,1536]{2,0,1:T(8,128)S(1)} all-to-all(f32[64,8,1536]{2,0,1:T(8,128)S(1)} %copy.39), channel_id=1, replica_groups=mesh['grp'=8,'blk'=16] {'grp'}, dimensions={1} | all-to-all | bytes 6291456 | tf_op jit(solution)/shard_map/all_to_all | solution.py:50
  449.2 6.6 %fusion.12 = f32[12,64,1536]{2,0,1:T(8,128)S(1)} fusion(f32[64,8,1536]{2,0,1:T(8,128)S(1)} %all_to_all.10, f32[8,12]{1,0:T(8,128)S(1)} %dynamic-slice_reduce_fusion), kind=kOutput, calls=%fused_computation.14 | convolution fusion | flops 113246208 | bytes 7864704 | tf_op jit(solution)/shard_map/sr,bsp->rbp/dot_general | solution.py:51
  455.8 37.9 %bitcast_add_fusion = f32[12,64,1536]{2,1,0:T(8,128)} fusion(f32[12,64,1536]{2,0,1:T(8,128)S(1)} %fusion.12, f32[2,1024,1536,1]{2,0,1,3:T(2,128)S(1)} %bitcast.56, f32[2,1024,12,64]{1,3,2,0:T(8,128)} %copy-done.6, f32[1024]{0:T(1024)S(1)} %all-reduce.1, f32[12,64,2]{1,0,2:T(8,128)S(1)} %broadcast_subtract_fusion), kind=kOutput, calls=%fused_computation.10 | convolution fusion | flops 28995354624 | bytes 28321792 | tf_op jit(solution)/shard_map/iajb,jbp->iap/dot_general | solution.py:43
  (32 shorter events, 0.2 us)
Async XLA Ops:
  6.5 97.8 %copy-start = (f32[96]{0:T(128)S(1)}, f32[96]{0:T(128)}, u32[]{:S(2)}) copy-start(f32[96]{0:T(128)} %param.8) | copy-start | bytes 1156
  42.9 49.7 %copy-start.5 = (u32[128]{0:T(128)S(1)}, u32[128]{0:T(128)}, u32[]{:S(2)}) copy-start(u32[128]{0:T(128)} %constant.36) | copy-start | bytes 1540
  42.9 50.3 %copy-start.4 = (u32[128]{0:T(128)S(1)}, u32[128]{0:T(128)}, u32[]{:S(2)}) copy-start(u32[128]{0:T(128)} %constant.31) | copy-start | bytes 1540
  42.9 51.6 %copy-start.3 = (s32[12]{0:T(128)S(1)}, s32[12]{0:T(128)}, u32[]{:S(2)}) copy-start(s32[12]{0:T(128)} %param.7) | copy-start | bytes 148
  42.9 62.4 %copy-start.2 = (f32[64]{0:T(128)S(1)}, f32[64]{0:T(128)}, u32[]{:S(2)}) copy-start(f32[64]{0:T(128)} %param.9) | copy-start | bytes 772
  42.9 44.5 %all-to-all-start = ((f32[8,64,1536]{2,1,0:T(8,128)}), f32[8,64,1536]{2,1,0:T(8,128)S(1)}, u32[]{:S(2)}, u32[]{:S(2)}) async-start(f32[8,64,1536]{2,1,0:T(8,128)} %copy.34), calls=%async_computation | async-start | bytes 6291456 | tf_op jit(solution)/shard_map/all_to_all | solution.py:23
  46.7 115.6 %all-gather.4.cloned.1.call-start = ((), (), s32[]{:S(2)}) async-start(), calls=%async_computation.2 | async-start | bytes 13369344 | tf_op jit(solution)/shard_map/all_gather | solution.py:33
  92.5 110.2 %slice-start = ((s8[4718592]{0:T(1024)(128)(4,1)}), s8[524288]{0:T(1024)(128)(4,1)S(1)}, s32[]{:S(2)}) async-start(s8[4718592]{0:T(1024)(128)(4,1)} %bitcast.48), calls=%async_computation.4 | async-start | bytes 1048576
  92.5 305.4 %all-reduce.4.cloned.1.call-start = ((), (), s32[]{:S(2)}) async-start(), calls=%async_computation.3 | async-start | bytes 25165824 | tf_op jit(solution)/shard_map/psum | solution.py:47
  162.2 40.5 %slice-start.1 = ((s8[4718592]{0:T(1024)(128)(4,1)}), s8[4194304]{0:T(1024)(128)(4,1)S(1)}, s32[]{:S(2)}) async-start(s8[4718592]{0:T(1024)(128)(4,1)} %bitcast.48), calls=%async_computation.5 | async-start | bytes 8388608
  200.1 2.6 copy-start.6
  399.1 56.7 %slice-start.2 = ((s8[12582912]{0:T(1024)(128)(4,1)}), s8[4194304]{0:T(1024)(128)(4,1)S(1)}, s32[]{:S(2)}) async-start(s8[12582912]{0:T(1024)(128)(4,1)} %bitcast.54), calls=%async_computation.6 | async-start | bytes 8388608
  402.9 52.9 %slice-start.3 = ((s8[12582912]{0:T(1024)(128)(4,1)}), s8[4194304]{0:T(1024)(128)(4,1)S(1)}, s32[]{:S(2)}) async-start(s8[12582912]{0:T(1024)(128)(4,1)} %bitcast.54), calls=%async_computation.7 | async-start | bytes 8388608
  449.2 6.6 %slice-start.4 = ((s8[12582912]{0:T(1024)(128)(4,1)}), s8[4194304]{0:T(1024)(128)(4,1)S(1)}, s32[]{:S(2)}) async-start(s8[12582912]{0:T(1024)(128)(4,1)} %bitcast.54), calls=%async_computation.8 | async-start | bytes 8388608
  455.8 37.9 %copy-start.1 = (f32[96]{0:T(128)S(1)}, f32[96]{0:T(128)}, u32[]{:S(2)}) copy-start(f32[96]{0:T(128)} %param.8) | copy-start | bytes 1156
Sparse Core Ops, SparseCore 0:
  92.6 69.5 all-gather.3
  237.9 160.0 all-reduce.3
where the time goes:
time: 509 us; the launch traced here: 501 us
  waiting for transfers between devices  228 us (45%)
  matrix products  135 us (27%)
  blocking collectives  107 us (21%)
  between operations  15.3 us (3%)
  local copies, waits for them, and re-layouts  11.1 us (2%)
    psum x1, waiting for transfers between devices, body(): summed = lax.psum(density_term, 'blk')  160 us
    all_to_all x1, blocking collectives, body(): lax.all_to_all(returning, 'grp', split_axis=1, concat_axis=1, tiled=True)  44.4 us
    all_to_all x1, waiting for transfers between devices, body(): lax.all_to_all(outgoing, 'grp', split_axis=0, concat_axis=0, tiled=True)  40.4 us
    unnamed x2, blocking collectives  38.6 us
    dot_general x1, matrix products, body(): jnp.einsum('iajb,jbp->iap', amplitude, blocks, precision=highest)  37.9 us
    dot_general x1, matrix products, body(): jnp.einsum('iap,jbp->iajb', integrals, blocks, precision=highest)  37.8 us
    dot_general x1, matrix products, body(): jnp.einsum('iajb,iap->bjp', amplitudes, integrals, precision=highest)  35 us
    all_gather x1, waiting for transfers between devices, body(): blocks = lax.all_gather(partner, 'blk', axis=1, tiled=True)  27.4 us
  transfers between devices with their start and end apart: 3, of which 3 were waited for; matrix products, arithmetic and copies ran while one was open for 0% of the time, Pallas kernels for 0%

commit v1 on v0

v1 whole, which is shorter than its diff:
```python
import jax
import jax.numpy as jnp
from jax import lax
from jax.experimental import pallas as pl
from jax.experimental.pallas import tpu as pltpu
from jax.sharding import PartitionSpec as P

MESH = pl.DeviceIdType.MESH
F32 = jnp.float32
BF16 = jnp.bfloat16
GROUPS = 8
BLOCKS = 16
OWN = 12
SLOTS = 2
WIDTH = 64
AUX = 1536
HELD = OWN * WIDTH
ALL = 2 * HELD
STACK = 2 * SLOTS * WIDTH
TILE = 256
CHUNKS = 2
PART = WIDTH // CHUNKS


def note_kernel(ints_ref, vir_ref, ints_out, vir_out, send_a, recv_a, send_b, recv_b, local):
    group = lax.axis_index("grp")
    block = lax.axis_index("blk")
    barrier = pltpu.get_barrier_semaphore()
    for step in range(1, GROUPS):
        pl.semaphore_signal(barrier, 1, device_id={"grp": lax.rem(group + step, GROUPS)}, device_id_type=MESH)
    for step in range(1, BLOCKS):
        pl.semaphore_signal(barrier, 1, device_id={"blk": lax.rem(block + step, BLOCKS)}, device_id_type=MESH)
    keep_a = pltpu.make_async_copy(ints_ref, ints_out.at[group], local.at[0])
    keep_b = pltpu.make_async_copy(vir_ref, vir_out.at[block], local.at[1])
    keep_a.start()
    keep_b.start()
    pl.semaphore_wait(barrier, GROUPS + BLOCKS - 2)

    def to_group(step, slot):
        return pltpu.make_async_remote_copy(
            ints_ref, ints_out.at[slot], send_a.at[step], recv_a.at[slot],
            device_id={"grp": lax.rem(group + step, GROUPS)}, device_id_type=MESH)

    def to_block(step, slot):
        return pltpu.make_async_remote_copy(
            vir_ref, vir_out.at[slot], send_b.at[step], recv_b.at[slot],
            device_id={"blk": lax.rem(block + step, BLOCKS)}, device_id_type=MESH)

    for step in range(1, GROUPS):
        to_group(step, group).start()
    for step in range(1, BLOCKS):
        to_block(step, block).start()
    keep_a.wait()
    keep_b.wait()
    for step in range(1, GROUPS):
        to_group(step, group).wait_send()
        to_group(step, lax.rem(group + step, GROUPS)).wait_recv()
    for step in range(1, BLOCKS):
        to_block(step, block).wait_send()
        to_block(step, lax.rem(block + step, BLOCKS)).wait_recv()


def exchange_notes(ints, vir):
    return pl.pallas_call(
        note_kernel,
        out_shape=(
            jax.ShapeDtypeStruct((GROUPS, 1, 128), jnp.int32),
            jax.ShapeDtypeStruct((BLOCKS, 1, 128), F32),
        ),
        in_specs=[pl.BlockSpec(memory_space=pltpu.VMEM)] * 2,
        out_specs=(pl.BlockSpec(memory_space=pltpu.VMEM),) * 2,
        scratch_shapes=[
            pltpu.SemaphoreType.DMA((GROUPS,)),
            pltpu.SemaphoreType.DMA((GROUPS,)),
            pltpu.SemaphoreType.DMA((BLOCKS,)),
            pltpu.SemaphoreType.DMA((BLOCKS,)),
            pltpu.SemaphoreType.DMA((2,)),
        ],
        compiler_params=pltpu.CompilerParams(collective_id=0, has_side_effects=True),
        name="notes",
    )(ints, vir)


def pick_kernel(_, rows_ref, out_ref):
    out_ref[...] = rows_ref[...]


def pick_rows(wanted, integrals):
    return pl.pallas_call(
        pick_kernel,
        out_shape=jax.ShapeDtypeStruct((GROUPS, WIDTH, AUX), F32),
        grid_spec=pltpu.PrefetchScalarGridSpec(
            num_scalar_prefetch=1,
            grid=(GROUPS,),
            in_specs=[pl.BlockSpec((1, WIDTH, AUX), lambda i, wanted: (wanted[i], 0, 0))],
            out_specs=pl.BlockSpec((1, WIDTH, AUX), lambda i, wanted: (i, 0, 0)),
        ),
        name="pick",
    )(wanted, integrals)


def split(values):
    high = values.astype(BF16)
    return high, (values - high.astype(F32)).astype(BF16)


def rows_of(slot, side, chunk=None):
    start = (slot * 2 + side) * WIDTH
    if chunk is None:
        return pl.ds(start, WIDTH)
    return pl.ds(start + chunk * PART, PART)


def main_kernel(
    sources, valid, picks, held_ref, outgoing, row_part, column_part,
    own_out, arrived,
    high, low, total, stack, travel, sums, landed, parts,
    side_send, side_land, home, other, got_a, got_b,
    swap_sem, fetch_send, fetch_recv, local_sem, side_a, side_b,
    hop_send, hop_recv, sum_send, sum_recv, back_a, back_b,
    out_send, out_recv, own_sem,
):
    group = lax.axis_index("grp")
    block = lax.axis_index("blk")
    core = lax.rem(block, 2)
    level = lax.rem(block // 2, 4)
    side = block // 8
    twin = {"blk": block + 1 - 2 * core}
    across = {"blk": lax.rem(block + 8, 16)}
    ring = (
        {"blk": side * 8 + lax.rem(level + 1, 4) * 2 + core},
        {"blk": side * 8 + lax.rem(level + 3, 4) * 2 + core},
    )
    got = (got_a, got_b)

    barrier = pltpu.get_barrier_semaphore()
    for peer in (twin, across, ring[0], ring[1]):
        pl.semaphore_signal(barrier, 1, device_id=peer, device_id_type=MESH)
    for step in range(1, GROUPS):
        pl.semaphore_signal(barrier, 1, device_id={"grp": lax.rem(group + step, GROUPS)}, device_id_type=MESH)

    keep = pltpu.make_async_copy(held_ref, total.at[pl.ds(0, HELD)], local_sem.at[CHUNKS])
    keep.start()
    keep_own = [
        pltpu.make_async_copy(outgoing.at[group, pl.ds(c * PART, PART)], got[c].at[group], local_sem.at[c])
        for c in range(CHUNKS)
    ]
    for copy in keep_own:
        copy.start()
    pl.semaphore_wait(barrier, GROUPS + 3)

    def remote(src, dst, send, recv, peer):
        return pltpu.make_async_remote_copy(src, dst, send, recv, device_id=peer, device_id_type=MESH)

    def fetch(step, c, slot):
        peer = lax.rem(group + step, GROUPS)
        return remote(outgoing.at[peer, pl.ds(c * PART, PART)], got[c].at[slot],
                      fetch_send.at[c, step], fetch_recv.at[c, slot], {"grp": peer})

    swap = remote(held_ref, total.at[pl.ds(HELD, HELD)], swap_sem.at[0], swap_sem.at[1], twin)
    for c in range(CHUNKS):
        for step in range(1, GROUPS):
            fetch(step, c, group).start()
        if c == 0:
            swap.start()

    def prepare(first):
        def tile(index, carry):
            rows = pl.ds(pl.multiple_of(first + index * 64, 64), 64)
            upper, lower = split(total[rows, :])
            high[rows, :] = upper
            low[rows, :] = lower
            total[rows, :] = jnp.zeros((64, AUX), F32)
            return carry
        lax.fori_loop(0, HELD // 64, tile, 0)

    keep.wait()
    prepare(0)

    def beside(slot, c):
        return remote(stack.at[0, rows_of(slot, 0, c)], stack.at[0, rows_of(slot, 1, c)],
                      side_a.at[slot, c], side_b.at[slot, c], across)

    def hop(step, slot, part, c):
        return remote(stack.at[step, rows_of(slot, part, c)], stack.at[step + 1, rows_of(slot, part, c)],
                      hop_send.at[step, slot, part, c], hop_recv.at[step, slot, part, c], ring[slot])

    for c in range(CHUNKS):
        keep_own[c].wait()
        for step in range(1, GROUPS):
            fetch(step, c, lax.rem(group + step, GROUPS)).wait_recv()
        for slot in range(SLOTS):
            stack[0, rows_of(slot, 0, c), :] = got[c][sources[slot]] * valid[slot]
        for slot in range(SLOTS):
            beside(slot, c).start()
            hop(0, slot, 0, c).start()
        if c == 0:
            swap.wait()
            prepare(HELD)
    for c in range(CHUNKS):
        for slot in range(SLOTS):
            beside(slot, c).wait_recv()
            hop(0, slot, 1, c).start()

    def sum_hop(step, slot, part, c):
        return remote(sums.at[step, rows_of(slot, part, c)], landed.at[step - 1, rows_of(slot, part, c)],
                      sum_send.at[step, slot, part, c], sum_recv.at[step, slot, part, c], ring[slot])

    pieces = [(slot, part, c) for part in (0, 1) for c in range(CHUNKS) for slot in range(SLOTS)]
    sum_pieces = [(slot, part, c) for part in (1, 0) for c in range(CHUNKS) for slot in range(SLOTS)]

    def stage(step, carry):
        @pl.when(step > 0)
        def _():
            for slot, part, c in pieces:
                hop(step - 1, slot, part, c).wait_recv()

                @pl.when(step < 3)
                def _():
                    hop(step, slot, part, c).start()

        def cut(index, carry):
            rows = pl.ds(pl.multiple_of(index * 64, 64), 64)
            upper, lower = split(stack[step, rows, :])
            travel[rows, :] = upper
            travel[pl.ds(pl.multiple_of(STACK + index * 64, 64), 64), :] = lower
            travel[pl.ds(pl.multiple_of(2 * STACK + index * 64, 64), 64), :] = upper
            sums[step, rows, :] = jnp.zeros((64, AUX), F32)
            return carry

        lax.fori_loop(0, STACK // 64, cut, 0)

        def tile(index, carry):
            rows = pl.ds(pl.multiple_of(index * TILE, TILE), TILE)
            nt = (((1,), (1,)), ((), ()))
            tn = (((0,), (0,)), ((), ()))
            upper = high[rows, :]
            lower = low[rows, :]
            near = travel[pl.ds(0, STACK), :]
            far = travel[pl.ds(STACK, STACK), :]
            pair = lax.dot_general(upper, near, nt, preferred_element_type=F32)
            pair += lax.dot_general(upper, far, nt, preferred_element_type=F32)
            pair += lax.dot_general(lower, near, nt, preferred_element_type=F32)
            amplitude = pair / (row_part[rows, :] + column_part[step])
            big, small = split(amplitude)
            total[rows, :] += jnp.dot(jnp.concatenate([big, big, small], axis=1), travel[...], preferred_element_type=F32)
            back = lax.dot_general(big, upper, tn, preferred_element_type=F32)
            back += lax.dot_general(big, lower, tn, preferred_element_type=F32)
            back += lax.dot_general(small, upper, tn, preferred_element_type=F32)
            sums[step] += back
            return carry

        lax.fori_loop(0, ALL // TILE, tile, 0)

        @pl.when(step > 0)
        def _():
            for slot, part, c in sum_pieces:
                @pl.when(step > 1)
                def _():
                    sum_hop(step - 1, slot, part, c).wait_recv()
                    rows = rows_of(slot, part, c)
                    sums[step, rows, :] += landed[step - 2, rows, :]
                sum_hop(step, slot, part, c).start()
        return carry

    lax.fori_loop(0, 4, stage, 0)

    give = remote(total.at[pl.ds(HELD, HELD)], other, own_sem.at[0], own_sem.at[1], twin)
    give.start()

    def cross(slot, c):
        rows = pl.ds(slot * WIDTH + c * PART, PART)
        return remote(side_send.at[rows], side_land.at[rows], back_a.at[slot, c], back_b.at[slot, c], across)

    for slot, part, c in sum_pieces:
        sum_hop(3, slot, part, c).wait_recv()
        rows = rows_of(slot, part, c)
        value = sums[0, rows, :] + landed[2, rows, :]
        if part == 1:
            side_send[pl.ds(slot * WIDTH + c * PART, PART), :] = value
            cross(slot, c).start()
        else:
            home[pl.ds(slot * WIDTH + c * PART, PART), :] = value

    def ship(step, c, slot):
        peer = lax.rem(group + step, GROUPS)
        return remote(got[c].at[peer], arrived.at[slot, pl.ds(c * PART, PART)],
                      out_send.at[c, step], out_recv.at[c, slot], {"grp": peer})

    stay = [
        pltpu.make_async_copy(got[c].at[group], arrived.at[group, pl.ds(c * PART, PART)], local_sem.at[c])
        for c in range(CHUNKS)
    ]
    for c in range(CHUNKS):
        ready = []
        for slot in range(SLOTS):
            cross(slot, c).wait_recv()
            rows = pl.ds(slot * WIDTH + c * PART, PART)
            home[rows, :] += side_land[rows, :]
        for step in range(1, GROUPS + 1):
            peer = lax.rem(group + step, GROUPS)
            got[c][peer] = (picks[0, peer] * home[pl.ds(c * PART, PART), :]
                            + picks[1, peer] * home[pl.ds(WIDTH + c * PART, PART), :])
            if step < GROUPS:
                ship(step, c, group).start()
        stay[c].start()

    give.wait()

    def merge(index, carry):
        rows = pl.ds(pl.multiple_of(index * 64, 64), 64)
        total[rows, :] += other[rows, :]
        return carry

    lax.fori_loop(0, HELD // 64, merge, 0)
    store = pltpu.make_async_copy(total.at[pl.ds(0, HELD)], own_out, local_sem.at[CHUNKS])
    store.start()
    for c in range(CHUNKS):
        for step in range(1, GROUPS):
            fetch(step, c, group).wait_send()
        for slot in range(SLOTS):
            beside(slot, c).wait_send()
            cross(slot, c).wait_send()
            for part in range(2):
                for step in range(3):
                    hop(step, slot, part, c).wait_send()
                    sum_hop(step + 1, slot, part, c).wait_send()
    for c in range(CHUNKS):
        stay[c].wait()
        for step in range(1, GROUPS):
            ship(step, c, group).wait_send()
            ship(step, c, lax.rem(group + step, GROUPS)).wait_recv()
    store.wait()


def run_main(sources, valid, picks, held, outgoing, row_part, column_part):
    smem = pl.BlockSpec(memory_space=pltpu.SMEM)
    vmem = pl.BlockSpec(memory_space=pltpu.VMEM)
    hbm = pl.BlockSpec(memory_space=pl.ANY)
    dma = pltpu.SemaphoreType.DMA
    return pl.pallas_call(
        main_kernel,
        out_shape=(
            jax.ShapeDtypeStruct((HELD, AUX), F32),
            jax.ShapeDtypeStruct((GROUPS, WIDTH, AUX), F32),
        ),
        in_specs=[smem, smem, smem, hbm, hbm, vmem, vmem],
        out_specs=(hbm, hbm),
        scratch_shapes=[
            pltpu.VMEM((ALL, AUX), BF16),
            pltpu.VMEM((ALL, AUX), BF16),
            pltpu.VMEM((ALL, AUX), F32),
            pltpu.VMEM((4, STACK, AUX), F32),
            pltpu.VMEM((3 * STACK, AUX), BF16),
            pltpu.VMEM((4, STACK, AUX), F32),
            pltpu.VMEM((3, STACK, AUX), F32),
            pltpu.VMEM((8, 128), F32),
            pltpu.VMEM((SLOTS * WIDTH, AUX), F32),
            pltpu.VMEM((SLOTS * WIDTH, AUX), F32),
            pltpu.VMEM((SLOTS * WIDTH, AUX), F32),
            pltpu.VMEM((HELD, AUX), F32),
            pltpu.VMEM((GROUPS, PART, AUX), F32),
            pltpu.VMEM((GROUPS, PART, AUX), F32),
            dma((2,)),
            dma((CHUNKS, GROUPS)),
            dma((CHUNKS, GROUPS)),
            dma((CHUNKS + 1,)),
            dma((SLOTS, CHUNKS)),
            dma((SLOTS, CHUNKS)),
            dma((4, SLOTS, 2, CHUNKS)),
            dma((4, SLOTS, 2, CHUNKS)),
            dma((4, SLOTS, 2, CHUNKS)),
            dma((4, SLOTS, 2, CHUNKS)),
            dma((SLOTS, CHUNKS)),
            dma((SLOTS, CHUNKS)),
            dma((CHUNKS, GROUPS)),
            dma((CHUNKS, GROUPS)),
            dma((2,)),
        ],
        compiler_params=pltpu.CompilerParams(
            collective_id=1, has_side_effects=True, vmem_limit_bytes=64_000_000),
        name="main",
    )(sources, valid, picks, held, outgoing, row_part, column_part)


def join_kernel(wanted, present, own_ref, arrived_ref, out_ref):
    out_ref[...] = own_ref[...]
    for peer in range(GROUPS):
        @pl.when(present[peer] > 0)
        def _():
            out_ref[wanted[peer]] += arrived_ref[peer]


def join(wanted, present, own, arrived):
    height = 16
    return pl.pallas_call(
        join_kernel,
        out_shape=jax.ShapeDtypeStruct((OWN, WIDTH, AUX), F32),
        grid_spec=pltpu.PrefetchScalarGridSpec(
            num_scalar_prefetch=2,
            grid=(WIDTH // height,),
            in_specs=[
                pl.BlockSpec((OWN, height, AUX), lambda i, *_: (0, i, 0)),
                pl.BlockSpec((GROUPS, height, AUX), lambda i, *_: (0, i, 0)),
            ],
            out_specs=pl.BlockSpec((OWN, height, AUX), lambda i, *_: (0, i, 0)),
        ),
        name="join",
    )(wanted, present, own, arrived)


def body(integrals, pair_lists, row_orbital, occ_energy, vir_energy):
    group = lax.axis_index("grp")
    block = lax.axis_index("blk")
    core = block % 2
    level = (block // 2) % 4
    side = block // 8
    ints = jnp.concatenate([pair_lists[0], row_orbital, jnp.zeros((128 - SLOTS - OWN,), jnp.int32)])[None]
    vir = jnp.concatenate([vir_energy, jnp.zeros((128 - WIDTH,), F32)])[None]
    ints_all, vir_all = exchange_notes(ints, vir)
    lists = ints_all[:, 0, :SLOTS]
    orbitals = ints_all[:, 0, SLOTS:SLOTS + OWN]
    vir_all = vir_all[:, 0, :WIDTH]
    owners = lists // OWN
    offsets = lists % OWN
    match = owners == group
    wanted = jnp.sum(jnp.where(match, offsets, 0), axis=1).astype(jnp.int32)
    present = jnp.any(match, axis=1).astype(jnp.int32)
    outgoing = pick_rows(wanted, integrals)

    mine = lax.dynamic_index_in_dim(lists, group, 0, keepdims=False)
    sources = jnp.minimum(mine // OWN, GROUPS - 1).astype(jnp.int32)
    valid = (mine < GROUPS * OWN).astype(F32)
    picks = (mine[:, None] // OWN == jnp.arange(GROUPS)[None, :]).astype(F32)
    ids = jnp.arange(occ_energy.shape[0])
    row_energy = jnp.sum(jnp.where(orbitals.reshape(-1)[:, None] == ids, occ_energy, 0.0), axis=1)
    own_energy = lax.dynamic_slice_in_dim(row_energy, group * OWN, OWN, 0)
    partner_energy = jnp.sum(jnp.where(mine[:, None] == ids, row_energy, 0.0), axis=1)
    pair_vir = lax.dynamic_slice_in_dim(vir_all, block - core, 2, 0)
    twin_vir = jnp.where(core == 0, pair_vir[1], pair_vir[0])
    row_part = jnp.concatenate([
        own_energy[:, None] - vir_energy[None, :],
        own_energy[:, None] - twin_vir[None, :],
    ]).reshape(ALL, 1)
    grid = jnp.where(core == 0, vir_all.reshape(2, 4, 2, WIDTH)[:, :, 0], vir_all.reshape(2, 4, 2, WIDTH)[:, :, 1])
    grid = jnp.where(side == 0, grid, grid[::-1])
    up = jnp.stack([lax.dynamic_index_in_dim(grid, (level + 4 - k) % 4, 1, keepdims=False) for k in range(4)])
    down = jnp.stack([lax.dynamic_index_in_dim(grid, (level + k) % 4, 1, keepdims=False) for k in range(4)])
    column_part = jnp.stack([partner_energy[0] - up, partner_energy[1] - down], axis=1).reshape(4, 1, STACK)

    own, arrived = run_main(
        sources, valid, picks, integrals.reshape(HELD, AUX), outgoing, row_part, column_part)
    return join(wanted, present, own.reshape(OWN, WIDTH, AUX), arrived)


def solution(mesh):
    in_specs = (P("grp", "blk", None), P("grp", None), P("grp"), P(), P("blk"))
    out_specs = P("grp", "blk", None)
    return jax.shard_map(body, mesh=mesh, in_specs=in_specs, out_specs=out_specs, check_vma=False)
```

time: 509 us -> 258 us (0.51)
  Pallas kernels: 0 us -> 239 us
  waiting for transfers between devices: 228 us -> 0 us
  matrix products: 135 us -> 0 us
  blocking collectives: 107 us -> 0 us
  between operations: 15.3 us -> 0.08 us
  other arithmetic: 0.4 us -> 9.23 us
    pallas_call x0 -> x4, Pallas kernels: none -> 239 us  [the longest x1 213 us: run_main(): pl.pallas_call(main_kernel, out_shape=(jax.ShapeDtypeStruct((HELD, AUX),...]
    psum x1 -> x0, waiting for transfers between devices: 160 us -> none  [body(): summed = lax.psum(density_term, 'blk')]
    dot_general x9 -> x0, matrix products: 135 us -> none  [the longest x1 37.9 us: body(): jnp.einsum('iajb,jbp->iap', amplitude, blocks, precision=highest)]
    all_to_all x1 -> x0, blocking collectives: 44.4 us -> none  [body(): lax.all_to_all(returning, 'grp', split_axis=1, concat_axis=1, tiled=True)]
    all_to_all x1 -> x0, waiting for transfers between devices: 40.4 us -> none  [body(): lax.all_to_all(outgoing, 'grp', split_axis=0, concat_axis=0, tiled=True)]
    unnamed x2 -> x0, blocking collectives: 38.6 us -> none
    all_gather x1 -> x0, waiting for transfers between devices: 27.4 us -> none  [body(): blocks = lax.all_gather(partner, 'blk', axis=1, tiled=True)]
    all_gather x1 -> x0, blocking collectives: 23.9 us -> none  [body(): lax.all_gather(pair_lists, 'grp', axis=0, tiled=True)]
  transfers between devices with their start and end apart: 3 -> 0, of which waited for: 3 -> 0; matrix products, arithmetic and copies ran while one was open for 0% -> 0% of each run, Pallas kernels for 0% -> 0%
where the time goes in v1:
time: 258 us; the launch traced here: 255 us
  Pallas kernels  239 us (93%)
  other arithmetic  9.23 us (4%)
  local copies, waits for them, and re-layouts  6.22 us (2%)
    pallas_call x1, Pallas kernels, run_main(): pl.pallas_call(main_kernel, out_shape=(jax.ShapeDtypeStruct((HELD, AUX),...  213 us
    pallas_call x1, Pallas kernels, exchange_notes(): pl.pallas_call(note_kernel, out_shape=(jax.ShapeDtypeStruct((GROUPS, 1, 1...  13.9 us
    pallas_call x1, Pallas kernels, join(): pl.pallas_call(join_kernel, out_shape=jax.ShapeDtypeStruct((OWN, WIDTH, A...  6.45 us
    pallas_call x1, Pallas kernels, pick_rows(): pl.pallas_call(pick_kernel, out_shape=jax.ShapeDtypeStruct((GROUPS, WIDTH...  5.78 us

profile of v1, /device:TPU:0, one launch (start us, length us, event | category | flops | bytes accessed | tf_op | source)
XLA Modules:
  0.0 254.7 jit_solution(11587946603724072684)
XLA Ops:
  0.0 1.2 pad_bitcast_fusion.vir_ref
  1.2 1.3 add_bitcast_fusion.ints_ref
  2.5 13.9 %notes.1 = (s32[8,1,128]{2,1,0:T(1,128)}, f32[16,1,128]{2,1,0:T(1,128)}) custom-call(s32[1,128]{1,0:T(1,128)} %add_bitcast_fusion.ints_ref, f32[1,128]{1,0:T(1,128)} %pad_bitcast_fusion.vir_ref), custom_call_target="tpu_custom_call" | custom-call | tf_op jit(solution)/shard_map/notes/pallas_call | solution.py:64
  16.3 0.7 fusion.15
  17.0 0.8 fusion.20
  17.9 0.7 sign_compare_fusion
  18.6 0.1 copy.23
  18.7 0.8 slice_reduce_fusion
  19.4 0.1 eq.72
  19.5 0.8 select_reduce_fusion
  20.3 0.1 dynamic_slice.30
  20.4 0.7 fusion.21
  21.1 0.5 compare_convert_fusion.1
  21.7 0.2 fusion.7
  21.9 0.6 broadcast_minimum_fusion
  22.4 0.7 fusion.22
  23.1 0.1 copy.25
  23.2 0.6 compare_convert_fusion.picks
  23.8 0.1 copy.27
  23.9 0.5 fusion.14._.wanted
  24.4 0.5 convert_element_type.9.present
  24.9 1.3 fusion.1
  26.3 0.7 reshape.203.column_part
  27.0 0.7 broadcast_subtract_fusion.1
  27.7 1.7 reshape.205.row_part
  29.4 5.8 %pick.1.outgoing = f32[8,64,1536]{2,1,0:T(8,128)} custom-call(s32[8]{0:T(128)} %fusion.14._.wanted, f32[12,64,1536]{2,1,0:T(8,128)} %rows_ref.1), custom_call_target="tpu_custom_call" | custom-call | tf_op jit(solution)/shard_map/pick/pallas_call | solution.py:89
  35.2 213.1 %main.1 = (f32[768,1536]{1,0:T(8,128)}, f32[8,64,1536]{2,1,0:T(8,128)}) custom-call(s32[2]{0:T(128)} %get-tuple-element.15.sources, f32[2]{0:T(128)} %get-tuple-element.13.valid, f32[2,8]{1,0:T(2,128)} %compare_convert_fusion.picks, f32[768,1536]{1,0:T(8,128)} %bitcast.51, f32[8,64,1536]{2,1,0:T(8,128)} %pick.1.outgoing, f32[1536,1]{1,0:T(8,128)} %reshape.205.row_part, ...), custom_call_target="tpu_custom_call" | custom-call | tf_op jit(solution)/shard_map/main/pallas_call | solution.py:341
  248.2 6.5 %join.1 = f32[12,64,1536]{2,1,0:T(8,128)} custom-call(s32[8]{0:T(128)} %fusion.14._.wanted, s32[8]{0:T(128)} %convert_element_type.9.present, f32[12,64,1536]{2,1,0:T(8,128)} %bitcast.52, f32[8,64,1536]{2,1,0:T(8,128)} %get-tuple-element.12.arrived_ref), custom_call_target="tpu_custom_call" | custom-call | tf_op jit(solution)/shard_map/join/pallas_call | solution.py:396
  (8 shorter events, 0.1 us)

commit v2 on v0

v2 whole, which is shorter than its diff:
```python
import jax
import jax.numpy as jnp
from jax import lax
from jax.experimental import pallas as pl
from jax.experimental.pallas import tpu as pltpu
from jax.sharding import PartitionSpec as P

MESH = pl.DeviceIdType.MESH
F32 = jnp.float32
BF16 = jnp.bfloat16
GROUPS = 8
BLOCKS = 16
OWN = 12
SLOTS = 2
WIDTH = 64
AUX = 1536
HELD = OWN * WIDTH
ALL = 2 * HELD
CHUNKS = 4
PART = WIDTH // CHUNKS
HALF = WIDTH // 2
STEP_ROWS = 2 * SLOTS * HALF
STACK = 2 * STEP_ROWS
TILE = 512
TILES = ALL // TILE
LANES = 128
NT = (((1,), (1,)), ((), ()))
TN = (((0,), (0,)), ((), ()))
CALL_OF = {(0, 0): (0, 0), (0, 1): (0, 1), (0, 2): (1, 0), (0, 3): (1, 1),
           (1, 1): (2, 0), (1, 2): (2, 1), (1, 3): (3, 0), (1, 0): (3, 1)}


def split(values):
    high = values.astype(BF16)
    return high, (values - high.astype(F32)).astype(BF16)


def step_rows(slot, part, c):
    return pl.ds((slot * 2 + part) * HALF + (c % 2) * PART, PART)


def sum_place(step, slot, part, c):
    call, half = CALL_OF[(c // 2, step)]
    return call, pl.ds(half * STEP_ROWS + (slot * 2 + part) * HALF + (c % 2) * PART, PART)


def main_kernel(
    lists_ref, orbitals_ref, occ_ref, vir_ref, held_ref,
    own_out, arrived, flags,
    ints_mine, ints_all, vir_mine, vir_all, ints,
    high, low, total, stack, travel, amp, sums, landed,
    side_send, side_land, home, other, row_part, column_part,
    got_0, got_1, got_2, got_3, box_0, box_1, box_2, box_3,
    note_a, note_b, note_c, note_d, local_sem, swap_sem,
    fetch_send, fetch_recv, side_a, side_b,
    hop_send, hop_recv, sum_send, sum_recv, back_a, back_b,
    out_send, out_recv, own_sem,
):
    group = lax.axis_index("grp")
    block = lax.axis_index("blk")
    core = lax.rem(block, 2)
    level = lax.rem(block // 2, 4)
    side = block // 8
    twin_block = block + 1 - 2 * core
    twin = {"blk": twin_block}
    across = {"blk": lax.rem(block + 8, 16)}
    ring = (
        {"blk": side * 8 + lax.rem(level + 1, 4) * 2 + core},
        {"blk": side * 8 + lax.rem(level + 3, 4) * 2 + core},
    )
    got = (got_0, got_1, got_2, got_3)
    box = (box_0, box_1, box_2, box_3)

    barrier = pltpu.get_barrier_semaphore()
    for step in range(1, GROUPS):
        pl.semaphore_signal(barrier, 1, device_id={"grp": lax.rem(group + step, GROUPS)}, device_id_type=MESH)
    for step in range(1, BLOCKS):
        pl.semaphore_signal(barrier, 1, device_id={"blk": lax.rem(block + step, BLOCKS)}, device_id_type=MESH)

    keep = pltpu.make_async_copy(held_ref, other, local_sem.at[0])
    keep.start()
    lane = lax.broadcasted_iota(jnp.int32, (1, LANES), 1)
    row = jnp.zeros((1, LANES), jnp.int32)
    for j in range(SLOTS):
        row = jnp.where(lane == j, lists_ref[0, j], row)
    for j in range(OWN):
        row = jnp.where(lane == SLOTS + j, orbitals_ref[j], row)
    ints_mine[...] = row
    ints_all[group] = row
    vir = vir_ref[...]
    vir_row = jnp.concatenate([vir[:, :HALF]] * 8 + [vir[:, HALF:]] * 8, axis=1)
    vir_mine[...] = vir_row
    vir_all[block] = vir_row
    pl.semaphore_wait(barrier, GROUPS + BLOCKS - 2)

    def remote(src, dst, send, recv, peer):
        return pltpu.make_async_remote_copy(src, dst, send, recv, device_id=peer, device_id_type=MESH)

    def to_group(step, slot):
        return remote(ints_mine, ints_all.at[slot], note_a.at[step], note_b.at[slot],
                      {"grp": lax.rem(group + step, GROUPS)})

    def to_block(step, slot):
        return remote(vir_mine, vir_all.at[slot], note_c.at[step], note_d.at[slot],
                      {"blk": lax.rem(block + step, BLOCKS)})

    for step in range(1, GROUPS):
        to_group(step, group).start()
    for step in range(1, BLOCKS):
        to_block(step, block).start()
    keep.wait()
    for step in range(1, GROUPS):
        to_group(step, lax.rem(group + step, GROUPS)).wait_recv()
    to_scalar = pltpu.make_async_copy(ints_all, ints, local_sem.at[1])
    to_scalar.start()
    to_scalar.wait()

    wanted = []
    for peer in range(GROUPS):
        place = jnp.int32(0)
        found = jnp.int32(0)
        for slot in range(SLOTS):
            listed = ints[peer, 0, slot]
            match = listed // OWN == group
            place = jnp.where(match, listed % OWN, place)
            found = jnp.where(match, 1, found)
        flags[0, peer] = place
        flags[1, peer] = found

    def fetch(step, c, slot):
        peer = lax.rem(group + step, GROUPS)
        return remote(box[c].at[step], got[c].at[slot],
                      fetch_send.at[c, step], fetch_recv.at[c, slot], {"grp": peer})

    def fill(c):
        for step in range(GROUPS):
            peer = lax.rem(group + step, GROUPS)
            values = other[flags[0, peer], pl.ds(c * PART, PART), :]
            if step == 0:
                got[c][group] = values
            else:
                box[c][step] = values

    fill(0)
    for c in range(CHUNKS):
        if c + 1 < CHUNKS:
            fill(c + 1)
        for step in range(1, GROUPS):
            fetch(step, c, group).start()

    swap = remote(held_ref, total.at[pl.ds(OWN, OWN)], swap_sem.at[0], swap_sem.at[1], twin)

    def prepare(source, first):
        def tile(index, carry):
            rows = pl.ds(pl.multiple_of((first + index) * WIDTH, WIDTH), WIDTH)
            upper, lower = split(source[index + (first if source is total else 0)])
            high[rows, :] = upper
            low[rows, :] = lower
            total[first + index] = jnp.zeros((WIDTH, AUX), F32)
            return carry
        lax.fori_loop(0, OWN, tile, 0)

    prepare(other, 0)
    swap.start()

    mine = [ints[group, 0, slot] for slot in range(SLOTS)]
    sources = [jnp.minimum(row // OWN, GROUPS - 1) for row in mine]
    valid = [jnp.where(row < GROUPS * OWN, jnp.float32(1), jnp.float32(0)) for row in mine]
    partner_energy = [
        occ_ref[ints[sources[slot], 0, SLOTS + mine[slot] % OWN]] for slot in range(SLOTS)
    ]
    for step in range(1, BLOCKS):
        to_block(step, lax.rem(block + step, BLOCKS)).wait_recv()
    square = (lax.broadcasted_iota(jnp.int32, (HALF, HALF), 0)
              == lax.broadcasted_iota(jnp.int32, (HALF, HALF), 1))
    for owner, place in ((block, 0), (twin_block, 1)):
        for h in range(2):
            line = vir_all[owner, :, pl.ds(h * STACK, LANES)][:, :HALF]
            column = jnp.sum(jnp.where(square, line, 0.0), axis=1, keepdims=True)
            for i in range(OWN):
                energy = occ_ref[ints[group, 0, SLOTS + i]]
                row_part[pl.ds((place * OWN + i) * WIDTH + h * HALF, HALF), :] = energy - column
    piece = lax.broadcasted_iota(jnp.int32, (1, STACK), 1) // HALF
    for at_call in range(4):
        terms = jnp.zeros((1, STACK), F32)
        for (h, step), (call, half) in CALL_OF.items():
            if call != at_call:
                continue
            for slot in range(SLOTS):
                for part in range(2):
                    from_level = lax.rem(level + (4 - step if slot == 0 else step), 4)
                    from_side = side + part - 2 * part * side
                    line = vir_all[from_side * 8 + from_level * 2 + core, :, pl.ds(h * STACK, STACK)]
                    here = piece == half * 4 + slot * 2 + part
                    terms = jnp.where(here, partner_energy[slot] - line, terms)
        column_part[at_call] = terms

    def beside(slot, c):
        return remote(stack.at[c // 2, 0, step_rows(slot, 0, c)], stack.at[c // 2, 0, step_rows(slot, 1, c)],
                      side_a.at[slot, c], side_b.at[slot, c], across)

    def hop(step, slot, part, c):
        rows = step_rows(slot, part, c)
        return remote(stack.at[c // 2, step, rows], stack.at[c // 2, step + 1, rows],
                      hop_send.at[step, slot, part, c], hop_recv.at[step, slot, part, c], ring[slot])

    def sum_hop(step, slot, part, c):
        call, rows = sum_place(step, slot, part, c)
        return remote(sums.at[call, rows], landed.at[c // 2, step - 1, step_rows(slot, part, c)],
                      sum_send.at[step - 1, slot, part, c], sum_recv.at[step - 1, slot, part, c], ring[slot])

    def home_rows(slot, c):
        return pl.ds(slot * WIDTH + c * PART, PART)

    def cross(slot, c):
        rows = home_rows(slot, c)
        return remote(side_send.at[rows], side_land.at[rows], back_a.at[slot, c], back_b.at[slot, c], across)

    def ship(step, c, slot):
        return remote(box[c].at[step], arrived.at[slot, pl.ds(c * PART, PART)],
                      out_send.at[c, step], out_recv.at[c, slot], {"grp": lax.rem(group + step, GROUPS)})

    def stay(c):
        return pltpu.make_async_copy(box[c].at[0], arrived.at[group, pl.ds(c * PART, PART)], local_sem.at[2 + c])

    def on_fetch(c):
        for step in range(1, GROUPS):
            fetch(step, c, lax.rem(group + step, GROUPS)).wait_recv()
        for slot in range(SLOTS):
            stack[c // 2, 0, step_rows(slot, 0, c), :] = got[c][sources[slot]] * valid[slot]
        for slot in range(SLOTS):
            beside(slot, c).start()
            hop(0, slot, 0, c).start()

    def on_side(c):
        for slot in range(SLOTS):
            beside(slot, c).wait_recv()
            hop(0, slot, 1, c).start()

    def on_hop(step, part, c):
        for slot in range(SLOTS):
            hop(step - 1, slot, part, c).wait_recv()
            if step < 3:
                hop(step, slot, part, c).start()

    def on_sum(step, c):
        for part in (1, 0):
            for slot in range(SLOTS):
                if step > 1:
                    sum_hop(step - 1, slot, part, c).wait_recv()
                    call, rows = sum_place(step, slot, part, c)
                    sums[call, rows, :] += landed[c // 2, step - 2, step_rows(slot, part, c), :]
        for part in (1, 0):
            for slot in range(SLOTS):
                sum_hop(step, slot, part, c).start()

    def on_home(c):
        for part in (1, 0):
            for slot in range(SLOTS):
                sum_hop(3, slot, part, c).wait_recv()
                call, rows = sum_place(0, slot, part, c)
                value = sums[call, rows, :] + landed[c // 2, 2, step_rows(slot, part, c), :]
                (side_send if part else home)[home_rows(slot, c), :] = value
            if part:
                for slot in range(SLOTS):
                    cross(slot, c).start()

    def on_cross(c):
        for step in range(1, GROUPS):
            fetch(step, c, group).wait_send()
        for slot in range(SLOTS):
            cross(slot, c).wait_recv()
            home[home_rows(slot, c), :] += side_land[home_rows(slot, c), :]
        for step in range(GROUPS):
            peer = lax.rem(group + step, GROUPS)
            picks = [jnp.where(row // OWN == peer, jnp.float32(1), jnp.float32(0)) for row in mine]
            box[c][step] = picks[0] * home[home_rows(0, c), :] + picks[1] * home[home_rows(1, c), :]
        for step in range(1, GROUPS):
            ship(step, c, group).start()
        stay(c).start()

    on_fetch(0)
    swap.wait()
    prepare(total, OWN)
    on_side(0)
    on_hop(1, 0, 0)
    on_hop(1, 1, 0)
    on_hop(2, 0, 0)
    on_fetch(1)
    on_side(1)
    on_hop(2, 1, 0)
    on_hop(1, 0, 1)
    on_hop(1, 1, 1)

    open_events = {
        1: [lambda: on_sum(1, 0), lambda: on_sum(1, 1), lambda: on_hop(2, 0, 2),
            lambda: on_hop(3, 0, 0), lambda: on_hop(3, 1, 0), lambda: on_hop(3, 0, 1), lambda: on_hop(3, 1, 1)],
        2: [lambda: on_hop(2, 1, 3), lambda: on_sum(2, 0), lambda: on_sum(2, 1)],
        3: [lambda: on_sum(1, 2), lambda: on_sum(1, 3),
            lambda: on_hop(3, 0, 2), lambda: on_hop(3, 1, 2), lambda: on_hop(3, 0, 3), lambda: on_hop(3, 1, 3),
            lambda: on_home(0)],
    }
    pair_events = {
        (0, 2): [lambda: on_fetch(2), lambda: on_hop(2, 0, 1)],
        (1, 2): [lambda: on_fetch(3), lambda: on_hop(2, 1, 2)],
        (3, 2): [lambda: on_home(1), lambda: on_sum(2, 2)],
    }
    back_events = {
        (0, 0): [lambda: on_side(2), lambda: on_hop(2, 1, 1), lambda: on_hop(1, 0, 2)],
        (0, 1): [lambda: on_hop(1, 1, 2)],
        (1, 0): [lambda: on_side(3), lambda: on_hop(1, 0, 3)],
        (1, 1): [lambda: on_hop(1, 1, 3), lambda: on_hop(2, 0, 3)],
        (2, 0): [lambda: on_sum(3, 0)],
        (2, 1): [lambda: on_sum(3, 1)],
        (3, 0): [lambda: on_cross(0)],
        (3, 1): [lambda: on_cross(1), lambda: on_sum(2, 3)],
    }

    def run(events, call, index):
        for (at_call, at_index), actions in events.items():
            @pl.when((call == at_call) & (index == at_index))
            def _():
                for action in actions:
                    action()

    def one_call(call, carry):
        for at_call, actions in open_events.items():
            @pl.when(call == at_call)
            def _():
                for action in actions:
                    action()

        h = call // 2
        first = (call % 2) * 2 + h
        second = (first + 1) % 4

        def cut(index, carry):
            for half, step in ((0, first), (1, second)):
                upper, lower = split(stack[h, step, pl.ds(pl.multiple_of(index * 64, 64), 64), :])
                start = half * STEP_ROWS + index * 64
                travel[pl.ds(pl.multiple_of(start, 64), 64), :] = upper
                travel[pl.ds(pl.multiple_of(STACK + start, 64), 64), :] = lower
                travel[pl.ds(pl.multiple_of(2 * STACK + start, 64), 64), :] = upper
                sums[call, pl.ds(pl.multiple_of(start, 64), 64), :] = jnp.zeros((64, AUX), F32)
            return carry

        lax.fori_loop(0, STEP_ROWS // 64, cut, 0)

        def pair_tile(index, carry):
            rows = pl.ds(pl.multiple_of(index * TILE, TILE), TILE)
            upper = high[rows, :]
            near = travel[pl.ds(0, STACK), :]
            pair = lax.dot_general(upper, near, NT, preferred_element_type=F32)
            pair += lax.dot_general(upper, travel[pl.ds(STACK, STACK), :], NT, preferred_element_type=F32)
            pair += lax.dot_general(low[rows, :], near, NT, preferred_element_type=F32)
            big, small = split(pair / (row_part[rows, :] + column_part[call]))
            amp[rows, pl.ds(0, STACK)] = big
            amp[rows, pl.ds(STACK, STACK)] = big
            amp[rows, pl.ds(2 * STACK, STACK)] = small
            run(pair_events, call, index)
            return carry

        lax.fori_loop(0, TILES, pair_tile, 0)

        def back_tile(index, carry):
            rows = pl.ds(pl.multiple_of(index * TILE, TILE), TILE)
            held = pl.ds(index * (TILE // WIDTH), TILE // WIDTH)
            forward = jnp.dot(amp[rows, :], travel[...], preferred_element_type=F32)
            total[held] += forward.reshape(TILE // WIDTH, WIDTH, AUX)
            upper = high[rows, :]
            big = amp[rows, pl.ds(0, STACK)]
            back = lax.dot_general(big, upper, TN, preferred_element_type=F32)
            back += lax.dot_general(big, low[rows, :], TN, preferred_element_type=F32)
            back += lax.dot_general(amp[rows, pl.ds(2 * STACK, STACK)], upper, TN, preferred_element_type=F32)
            sums[call] += back
            run(back_events, call, index)
            return carry

        lax.fori_loop(0, TILES, back_tile, 0)
        return carry

    lax.fori_loop(0, 4, one_call, 0)

    give = remote(total.at[pl.ds(OWN, OWN)], other, own_sem.at[0], own_sem.at[1], twin)
    on_sum(3, 2)
    give.start()
    on_home(2)
    on_sum(3, 3)
    on_cross(2)
    on_home(3)
    on_cross(3)
    give.wait()

    def merge(index, carry):
        total[index] += other[index]
        return carry

    lax.fori_loop(0, OWN, merge, 0)
    store = pltpu.make_async_copy(total.at[pl.ds(0, OWN)], own_out, local_sem.at[0])
    store.start()
    for step in range(1, GROUPS):
        to_group(step, group).wait_send()
    for step in range(1, BLOCKS):
        to_block(step, block).wait_send()
    for c in range(CHUNKS):
        for slot in range(SLOTS):
            beside(slot, c).wait_send()
            cross(slot, c).wait_send()
            for part in range(2):
                for step in range(3):
                    hop(step, slot, part, c).wait_send()
                    sum_hop(step + 1, slot, part, c).wait_send()
    for c in range(CHUNKS):
        stay(c).wait()
        for step in range(1, GROUPS):
            ship(step, c, group).wait_send()
            ship(step, c, lax.rem(group + step, GROUPS)).wait_recv()
    store.wait()


def run_main(lists, orbitals, occ, vir, held):
    smem = pl.BlockSpec(memory_space=pltpu.SMEM)
    vmem = pl.BlockSpec(memory_space=pltpu.VMEM)
    hbm = pl.BlockSpec(memory_space=pl.ANY)
    dma = pltpu.SemaphoreType.DMA
    chunk = pltpu.VMEM((GROUPS, PART, AUX), F32)
    return pl.pallas_call(
        main_kernel,
        out_shape=(
            jax.ShapeDtypeStruct((OWN, WIDTH, AUX), F32),
            jax.ShapeDtypeStruct((GROUPS, WIDTH, AUX), F32),
            jax.ShapeDtypeStruct((2, GROUPS), jnp.int32),
        ),
        in_specs=[smem, smem, smem, vmem, hbm],
        out_specs=(hbm, hbm, smem),
        scratch_shapes=[
            pltpu.VMEM((1, LANES), jnp.int32),
            pltpu.VMEM((GROUPS, 1, LANES), jnp.int32),
            pltpu.VMEM((1, 2 * STACK), F32),
            pltpu.VMEM((BLOCKS, 1, 2 * STACK), F32),
            pltpu.SMEM((GROUPS, 1, LANES), jnp.int32),
            pltpu.VMEM((ALL, AUX), BF16),
            pltpu.VMEM((ALL, AUX), BF16),
            pltpu.VMEM((2 * OWN, WIDTH, AUX), F32),
            pltpu.VMEM((2, 4, STEP_ROWS, AUX), F32),
            pltpu.VMEM((3 * STACK, AUX), BF16),
            pltpu.VMEM((ALL, 3 * STACK), BF16),
            pltpu.VMEM((4, STACK, AUX), F32),
            pltpu.VMEM((2, 3, STEP_ROWS, AUX), F32),
            pltpu.VMEM((SLOTS * WIDTH, AUX), F32),
            pltpu.VMEM((SLOTS * WIDTH, AUX), F32),
            pltpu.VMEM((SLOTS * WIDTH, AUX), F32),
            pltpu.VMEM((OWN, WIDTH, AUX), F32),
            pltpu.VMEM((ALL, 1), F32),
            pltpu.VMEM((4, 1, STACK), F32),
            chunk, chunk, chunk, chunk, chunk, chunk, chunk, chunk,
            dma((GROUPS,)),
            dma((GROUPS,)),
            dma((BLOCKS,)),
            dma((BLOCKS,)),
            dma((2 + CHUNKS,)),
            dma((2,)),
            dma((CHUNKS, GROUPS)),
            dma((CHUNKS, GROUPS)),
            dma((SLOTS, CHUNKS)),
            dma((SLOTS, CHUNKS)),
            dma((3, SLOTS, 2, CHUNKS)),
            dma((3, SLOTS, 2, CHUNKS)),
            dma((3, SLOTS, 2, CHUNKS)),
            dma((3, SLOTS, 2, CHUNKS)),
            dma((SLOTS, CHUNKS)),
            dma((SLOTS, CHUNKS)),
            dma((CHUNKS, GROUPS)),
            dma((CHUNKS, GROUPS)),
            dma((2,)),
        ],
        compiler_params=pltpu.CompilerParams(
            collective_id=0, has_side_effects=True, vmem_limit_bytes=66_000_000),
        name="main",
    )(lists, orbitals, occ, vir, held)


def join_kernel(flags, own_ref, arrived_ref, out_ref):
    out_ref[...] = own_ref[...]
    for peer in range(GROUPS):
        @pl.when(flags[1, peer] > 0)
        def _():
            out_ref[flags[0, peer]] += arrived_ref[peer]


def join(flags, own, arrived):
    height = 16
    return pl.pallas_call(
        join_kernel,
        out_shape=jax.ShapeDtypeStruct((OWN, WIDTH, AUX), F32),
        grid_spec=pltpu.PrefetchScalarGridSpec(
            num_scalar_prefetch=1,
            grid=(WIDTH // height,),
            in_specs=[
                pl.BlockSpec((OWN, height, AUX), lambda i, *_: (0, i, 0)),
                pl.BlockSpec((GROUPS, height, AUX), lambda i, *_: (0, i, 0)),
            ],
            out_specs=pl.BlockSpec((OWN, height, AUX), lambda i, *_: (0, i, 0)),
        ),
        name="join",
    )(flags, own, arrived)


def body(integrals, pair_lists, row_orbital, occ_energy, vir_energy):
    own, arrived, flags = run_main(
        pair_lists, row_orbital, occ_energy, vir_energy.reshape(1, WIDTH), integrals)
    return join(flags, own, arrived)


def solution(mesh):
    in_specs = (P("grp", "blk", None), P("grp", None), P("grp"), P(), P("blk"))
    out_specs = P("grp", "blk", None)
    return jax.shard_map(body, mesh=mesh, in_specs=in_specs, out_specs=out_specs, check_vma=False)
```

time: 509 us -> 195 us (0.38); the launches traced: 501 us -> 194 us
  waiting for transfers between devices: 228 us -> 0 us
  Pallas kernels: 0 us -> 194 us
  matrix products: 135 us -> 0 us
  blocking collectives: 107 us -> 0 us
  between operations: 15.3 us -> 0.01 us
  local copies, waits for them, and re-layouts: 11.1 us -> 0 us
    pallas_call x0 -> x2, Pallas kernels: none -> 194 us  [the longest x1 187 us: run_main(): pl.pallas_call(main_kernel, out_shape=(jax.ShapeDtypeStruct((OWN, WIDTH,...]
    psum x1 -> x0, waiting for transfers between devices: 160 us -> none  [body(): summed = lax.psum(density_term, 'blk')]
    dot_general x9 -> x0, matrix products: 135 us -> none  [the longest x1 37.9 us: body(): jnp.einsum('iajb,jbp->iap', amplitude, blocks, precision=highest)]
    all_to_all x1 -> x0, blocking collectives: 44.4 us -> none  [body(): lax.all_to_all(returning, 'grp', split_axis=1, concat_axis=1, tiled=True)]
    all_to_all x1 -> x0, waiting for transfers between devices: 40.4 us -> none  [body(): lax.all_to_all(outgoing, 'grp', split_axis=0, concat_axis=0, tiled=True)]
    unnamed x2 -> x0, blocking collectives: 38.6 us -> none
    all_gather x1 -> x0, waiting for transfers between devices: 27.4 us -> none  [body(): blocks = lax.all_gather(partner, 'blk', axis=1, tiled=True)]
    all_gather x1 -> x0, blocking collectives: 23.9 us -> none  [body(): lax.all_gather(pair_lists, 'grp', axis=0, tiled=True)]
  transfers between devices with their start and end apart: 3 -> 0, of which waited for: 3 -> 0; matrix products, arithmetic and copies ran while one was open for 0% -> 0% of each run, Pallas kernels for 0% -> 0%
where the time goes in v2:
time: 195 us; the launch traced here: 194 us
  Pallas kernels  194 us (99%)
    pallas_call x1, Pallas kernels, run_main(): pl.pallas_call(main_kernel, out_shape=(jax.ShapeDtypeStruct((OWN, WIDTH,...  187 us
    pallas_call x1, Pallas kernels, join(): pl.pallas_call(join_kernel, out_shape=jax.ShapeDtypeStruct((OWN, WIDTH, A...  6.45 us

profile of v2, /device:TPU:0, one launch (start us, length us, event | category | flops | bytes accessed | tf_op | source)
XLA Modules:
  0.0 193.5 jit_solution(3896888415972859246)
XLA Ops:
  0.0 187.1 %main.1 = (f32[12,64,1536]{2,1,0:T(8,128)}, f32[8,64,1536]{2,1,0:T(8,128)}, s32[2,8]{1,0:T(2,128)}) custom-call(s32[1,2]{1,0:T(1,128)} %lists_ref.1, s32[12]{0:T(128)} %orbitals_ref.1, f32[96]{0:T(128)} %occ_ref.1, f32[1,64]{1,0:T(1,128)} %bitcast.1, f32[12,64,1536]{2,1,0:T(8,128)} %held_ref.1), custom_call_target="tpu_custom_call" | custom-call | tf_op jit(solution)/shard_map/main/pallas_call | solution.py:427
  187.1 6.4 %join.1 = f32[12,64,1536]{2,1,0:T(8,128)} custom-call(s32[2,8]{1,0:T(2,128)} %get-tuple-element.8.flags, f32[12,64,1536]{2,1,0:T(8,128)} %get-tuple-element.9.own_ref, f32[8,64,1536]{2,1,0:T(8,128)} %get-tuple-element.10.arrived_ref), custom_call_target="tpu_custom_call" | custom-call | tf_op jit(solution)/shard_map/join/pallas_call | solution.py:493

commit v3 on v2

--- a/solution.py
+++ b/solution.py
@@ -50,14 +50,19 @@
     ints_mine, ints_all, vir_mine, vir_all, ints,
     high, low, total, stack, travel, amp, sums, landed,
     side_send, side_land, home, other, row_part, column_part,
+    near_land, near_back,
     got_0, got_1, got_2, got_3, box_0, box_1, box_2, box_3,
     note_a, note_b, note_c, note_d, local_sem, swap_sem,
     fetch_send, fetch_recv, side_a, side_b,
     hop_send, hop_recv, sum_send, sum_recv, back_a, back_b,
-    out_send, out_recv, own_sem,
+    out_send, out_recv, own_sem, near_a, near_b, far_a, far_b,
 ):
     group = lax.axis_index("grp")
     block = lax.axis_index("blk")
+    column = group // 2
+    upper_side = lax.rem(group, 2)
+    opposite = group + 1 - 2 * upper_side
+    facing = {"grp": opposite}
     core = lax.rem(block, 2)
     level = lax.rem(block // 2, 4)
     side = block // 8
@@ -115,38 +120,41 @@
     to_scalar.start()
     to_scalar.wait()
 
-    wanted = []
-    for peer in range(GROUPS):
-        place = jnp.int32(0)
-        found = jnp.int32(0)
-        for slot in range(SLOTS):
-            listed = ints[peer, 0, slot]
-            match = listed // OWN == group
-            place = jnp.where(match, listed % OWN, place)
-            found = jnp.where(match, 1, found)
-        flags[0, peer] = place
-        flags[1, peer] = found
-
-    def fetch(step, c, slot):
-        peer = lax.rem(group + step, GROUPS)
-        return remote(box[c].at[step], got[c].at[slot],
-                      fetch_send.at[c, step], fetch_recv.at[c, slot], {"grp": peer})
+    def held_by(step, turn):
+        return lax.rem(column + step, 4) * 2 + lax.rem(upper_side + turn, 2)
+
+    for x in range(4):
+        for turn in range(2):
+            peer = x * 2 + lax.rem(upper_side + turn, 2)
+            place = jnp.int32(0)
+            found = jnp.int32(0)
+            for slot in range(SLOTS):
+                listed = ints[peer, 0, slot]
+                match = listed // OWN == group
+                place = jnp.where(match, listed % OWN, place)
+                found = jnp.where(match, 1, found)
+            flags[0, x * 2 + turn] = place
+            flags[1, x * 2 + turn] = found
+
+    def fetch(step, c, x):
+        return remote(box[c].at[pl.ds(step * 2, 2)], got[c].at[pl.ds(x * 2, 2)],
+                      fetch_send.at[c, step], fetch_recv.at[c, x], {"grp": held_by(step, 0)})
 
     def fill(c):
-        for step in range(GROUPS):
-            peer = lax.rem(group + step, GROUPS)
-            values = other[flags[0, peer], pl.ds(c * PART, PART), :]
-            if step == 0:
-                got[c][group] = values
-            else:
-                box[c][step] = values
+        for step in range(4):
+            for turn in range(2):
+                values = other[flags[0, lax.rem(column + step, 4) * 2 + turn], pl.ds(c * PART, PART), :]
+                if step == 0:
+                    got[c][column * 2 + turn] = values
+                else:
+                    box[c][step * 2 + turn] = values
 
     fill(0)
     for c in range(CHUNKS):
         if c + 1 < CHUNKS:
             fill(c + 1)
-        for step in range(1, GROUPS):
-            fetch(step, c, group).start()
+        for step in range(1, 4):
+            fetch(step, c, column).start()
 
     swap = remote(held_ref, total.at[pl.ds(OWN, OWN)], swap_sem.at[0], swap_sem.at[1], twin)
 
@@ -164,8 +172,13 @@
     swap.start()
 
     mine = [ints[group, 0, slot] for slot in range(SLOTS)]
+    theirs = [ints[opposite, 0, slot] for slot in range(SLOTS)]
+    one, none = jnp.float32(1), jnp.float32(0)
     sources = [jnp.minimum(row // OWN, GROUPS - 1) for row in mine]
-    valid = [jnp.where(row < GROUPS * OWN, jnp.float32(1), jnp.float32(0)) for row in mine]
+    columns = [source // 2 for source in sources]
+    their_columns = [jnp.minimum(row // OWN, GROUPS - 1) // 2 for row in theirs]
+    level_with = [jnp.where((row < GROUPS * OWN) & (lax.rem(row // OWN, 2) == upper_side), one, none) for row in mine]
+    opposed = [jnp.where((row < GROUPS * OWN) & (lax.rem(row // OWN, 2) != upper_side), one, none) for row in mine]
     partner_energy = [
         occ_ref[ints[sources[slot], 0, SLOTS + mine[slot] % OWN]] for slot in range(SLOTS)
     ]
@@ -176,10 +189,10 @@
     for owner, place in ((block, 0), (twin_block, 1)):
         for h in range(2):
             line = vir_all[owner, :, pl.ds(h * STACK, LANES)][:, :HALF]
-            column = jnp.sum(jnp.where(square, line, 0.0), axis=1, keepdims=True)
+            upright = jnp.sum(jnp.where(square, line, 0.0), axis=1, keepdims=True)
             for i in range(OWN):
                 energy = occ_ref[ints[group, 0, SLOTS + i]]
-                row_part[pl.ds((place * OWN + i) * WIDTH + h * HALF, HALF), :] = energy - column
+                row_part[pl.ds((place * OWN + i) * WIDTH + h * HALF, HALF), :] = energy - upright
     piece = lax.broadcasted_iota(jnp.int32, (1, STACK), 1) // HALF
     for at_call in range(4):
         terms = jnp.zeros((1, STACK), F32)
@@ -209,25 +222,39 @@
         return remote(sums.at[call, rows], landed.at[c // 2, step - 1, step_rows(slot, part, c)],
                       sum_send.at[step - 1, slot, part, c], sum_recv.at[step - 1, slot, part, c], ring[slot])
 
-    def home_rows(slot, c):
+    def side_rows(slot, c):
         return pl.ds(slot * WIDTH + c * PART, PART)
 
     def cross(slot, c):
-        rows = home_rows(slot, c)
+        rows = side_rows(slot, c)
         return remote(side_send.at[rows], side_land.at[rows], back_a.at[slot, c], back_b.at[slot, c], across)
 
-    def ship(step, c, slot):
-        return remote(box[c].at[step], arrived.at[slot, pl.ds(c * PART, PART)],
-                      out_send.at[c, step], out_recv.at[c, slot], {"grp": lax.rem(group + step, GROUPS)})
+    def pass_on(c):
+        return remote(box[c].at[pl.ds(0, 2)], near_land.at[c], near_a.at[c], near_b.at[c], facing)
+
+    def pass_back(c):
+        return remote(home.at[c], near_back.at[c], far_a.at[c], far_b.at[c], facing)
+
+    def ship(step, c, x):
+        return remote(box[c].at[pl.ds(step * 2, 2)], arrived.at[pl.ds(x * 2, 2), pl.ds(c * PART, PART)],
+                      out_send.at[c, step], out_recv.at[c, x], {"grp": held_by(step, 0)})
 
     def stay(c):
-        return pltpu.make_async_copy(box[c].at[0], arrived.at[group, pl.ds(c * PART, PART)], local_sem.at[2 + c])
+        return pltpu.make_async_copy(
+            box[c].at[pl.ds(0, 2)], arrived.at[pl.ds(column * 2, 2), pl.ds(c * PART, PART)], local_sem.at[2 + c])
 
     def on_fetch(c):
-        for step in range(1, GROUPS):
-            fetch(step, c, lax.rem(group + step, GROUPS)).wait_recv()
-        for slot in range(SLOTS):
-            stack[c // 2, 0, step_rows(slot, 0, c), :] = got[c][sources[slot]] * valid[slot]
+        for step in range(1, 4):
+            fetch(step, c, lax.rem(column + step, 4)).wait_recv()
+        for slot in range(SLOTS):
+            box[c][slot] = got[c][their_columns[slot] * 2 + 1]
+        pass_on(c).start()
+
+    def on_pass(c):
+        pass_on(c).wait_recv()
+        for slot in range(SLOTS):
+            stack[c // 2, 0, step_rows(slot, 0, c), :] = (
+                got[c][columns[slot] * 2] * level_with[slot] + near_land[c, slot] * opposed[slot])
         for slot in range(SLOTS):
             beside(slot, c).start()
             hop(0, slot, 0, c).start()
@@ -260,75 +287,89 @@
                 sum_hop(3, slot, part, c).wait_recv()
                 call, rows = sum_place(0, slot, part, c)
                 value = sums[call, rows, :] + landed[c // 2, 2, step_rows(slot, part, c), :]
-                (side_send if part else home)[home_rows(slot, c), :] = value
+                if part:
+                    side_send[side_rows(slot, c), :] = value
+                else:
+                    home[c, slot] = value
             if part:
                 for slot in range(SLOTS):
                     cross(slot, c).start()
 
     def on_cross(c):
-        for step in range(1, GROUPS):
-            fetch(step, c, group).wait_send()
         for slot in range(SLOTS):
             cross(slot, c).wait_recv()
-            home[home_rows(slot, c), :] += side_land[home_rows(slot, c), :]
-        for step in range(GROUPS):
-            peer = lax.rem(group + step, GROUPS)
-            picks = [jnp.where(row // OWN == peer, jnp.float32(1), jnp.float32(0)) for row in mine]
-            box[c][step] = picks[0] * home[home_rows(0, c), :] + picks[1] * home[home_rows(1, c), :]
-        for step in range(1, GROUPS):
-            ship(step, c, group).start()
+            home[c, slot] += side_land[side_rows(slot, c), :]
+        pass_back(c).start()
+
+    def on_ship(c):
+        for step in range(1, 4):
+            fetch(step, c, column).wait_send()
+        pass_on(c).wait_send()
+
+        def blend(rows, source, step):
+            picks = [jnp.where(row // OWN == held_by(step, 0), one, none) for row in rows]
+            return picks[0] * source[c, 0] + picks[1] * source[c, 1]
+
+        for step in range(4):
+            box[c][step * 2] = blend(mine, home, step)
+        pass_back(c).wait_recv()
+        for step in range(4):
+            box[c][step * 2 + 1] = blend(theirs, near_back, step)
+        for step in range(1, 4):
+            ship(step, c, column).start()
         stay(c).start()
+
+    def play(*actions):
+        for action, *where in actions:
+            action(*where)
 
     on_fetch(0)
     swap.wait()
     prepare(total, OWN)
-    on_side(0)
-    on_hop(1, 0, 0)
-    on_hop(1, 1, 0)
-    on_hop(2, 0, 0)
-    on_fetch(1)
-    on_side(1)
-    on_hop(2, 1, 0)
-    on_hop(1, 0, 1)
-    on_hop(1, 1, 1)
+    play((on_pass, 0), (on_fetch, 1), (on_hop, 1, 0, 0), (on_side, 0), (on_pass, 1), (on_hop, 1, 1, 0),
+         (on_hop, 2, 0, 0), (on_fetch, 2), (on_hop, 1, 0, 1), (on_side, 1), (on_hop, 2, 1, 0), (on_hop, 2, 0, 1),
+         (on_pass, 2), (on_hop, 1, 1, 1))
 
     open_events = {
-        1: [lambda: on_sum(1, 0), lambda: on_sum(1, 1), lambda: on_hop(2, 0, 2),
-            lambda: on_hop(3, 0, 0), lambda: on_hop(3, 1, 0), lambda: on_hop(3, 0, 1), lambda: on_hop(3, 1, 1)],
-        2: [lambda: on_hop(2, 1, 3), lambda: on_sum(2, 0), lambda: on_sum(2, 1)],
-        3: [lambda: on_sum(1, 2), lambda: on_sum(1, 3),
-            lambda: on_hop(3, 0, 2), lambda: on_hop(3, 1, 2), lambda: on_hop(3, 0, 3), lambda: on_hop(3, 1, 3),
-            lambda: on_home(0)],
+        1: [(on_hop, 3, 0, 0), (on_hop, 3, 1, 0), (on_hop, 3, 0, 1), (on_hop, 3, 1, 1)],
+        3: [(on_hop, 3, 0, 2), (on_hop, 3, 1, 2), (on_hop, 3, 0, 3), (on_hop, 3, 1, 3)],
     }
     pair_events = {
-        (0, 2): [lambda: on_fetch(2), lambda: on_hop(2, 0, 1)],
-        (1, 2): [lambda: on_fetch(3), lambda: on_hop(2, 1, 2)],
-        (3, 2): [lambda: on_home(1), lambda: on_sum(2, 2)],
+        (0, 0): [(on_fetch, 3)],
+        (0, 1): [(on_hop, 1, 0, 2), (on_side, 2)],
+        (0, 2): [(on_hop, 2, 1, 1)],
+        (1, 1): [(on_hop, 2, 0, 3), (on_hop, 1, 1, 3)],
+        (3, 2): [(on_home, 0)],
     }
     back_events = {
-        (0, 0): [lambda: on_side(2), lambda: on_hop(2, 1, 1), lambda: on_hop(1, 0, 2)],
-        (0, 1): [lambda: on_hop(1, 1, 2)],
-        (1, 0): [lambda: on_side(3), lambda: on_hop(1, 0, 3)],
-        (1, 1): [lambda: on_hop(1, 1, 3), lambda: on_hop(2, 0, 3)],
-        (2, 0): [lambda: on_sum(3, 0)],
-        (2, 1): [lambda: on_sum(3, 1)],
-        (3, 0): [lambda: on_cross(0)],
-        (3, 1): [lambda: on_cross(1), lambda: on_sum(2, 3)],
+        (0, 1): [(on_hop, 2, 0, 2), (on_pass, 3)],
+        (0, 2): [(on_hop, 1, 1, 2), (on_sum, 1, 0), (on_sum, 1, 1)],
+        (1, 2): [(on_hop, 2, 1, 3), (on_sum, 2, 0), (on_sum, 2, 1)],
+        (2, 0): [(on_sum, 3, 0)],
+        (2, 2): [(on_sum, 3, 1), (on_sum, 1, 2), (on_sum, 1, 3)],
+        (3, 0): [(on_sum, 2, 2)],
+        (3, 1): [(on_home, 1)],
+        (3, 2): [(on_sum, 2, 3)],
+    }
+    own_events = {
+        (0, 1): [(on_hop, 1, 0, 3)],
+        (0, 2): [(on_hop, 2, 1, 2), (on_side, 3)],
+        (3, 0): [(on_cross, 0)],
+        (3, 1): [(on_cross, 1)],
+        (3, 2): [(on_ship, 0)],
     }
 
     def run(events, call, index):
         for (at_call, at_index), actions in events.items():
             @pl.when((call == at_call) & (index == at_index))
             def _():
-                for action in actions:
-                    action()
+                play(*actions)
 
     def one_call(call, carry):
         for at_call, actions in open_events.items():
             @pl.when(call == at_call)
             def _():
-                for action in actions:
-                    action()
+                play(*actions)
 
         h = call // 2
         first = (call % 2) * 2 + h
@@ -364,9 +405,6 @@
 
         def back_tile(index, carry):
             rows = pl.ds(pl.multiple_of(index * TILE, TILE), TILE)
-            held = pl.ds(index * (TILE // WIDTH), TILE // WIDTH)
-            forward = jnp.dot(amp[rows, :], travel[...], preferred_element_type=F32)
-            total[held] += forward.reshape(TILE // WIDTH, WIDTH, AUX)
             upper = high[rows, :]
             big = amp[rows, pl.ds(0, STACK)]
             back = lax.dot_general(big, upper, TN, preferred_element_type=F32)
@@ -377,6 +415,16 @@
             return carry
 
         lax.fori_loop(0, TILES, back_tile, 0)
+
+        def own_tile(index, carry):
+            rows = pl.ds(pl.multiple_of(index * TILE, TILE), TILE)
+            held = pl.ds(index * (TILE // WIDTH), TILE // WIDTH)
+            forward = jnp.dot(amp[rows, :], travel[...], preferred_element_type=F32)
+            total[held] += forward.reshape(TILE // WIDTH, WIDTH, AUX)
+            run(own_events, call, index)
+            return carry
+
+        lax.fori_loop(0, TILES, own_tile, 0)
         return carry
 
     lax.fori_loop(0, 4, one_call, 0)
@@ -384,11 +432,7 @@
     give = remote(total.at[pl.ds(OWN, OWN)], other, own_sem.at[0], own_sem.at[1], twin)
     on_sum(3, 2)
     give.start()
-    on_home(2)
-    on_sum(3, 3)
-    on_cross(2)
-    on_home(3)
-    on_cross(3)
+    play((on_sum, 3, 3), (on_ship, 1), (on_home, 2), (on_home, 3), (on_cross, 2), (on_cross, 3), (on_ship, 2), (on_ship, 3))
     give.wait()
 
     def merge(index, carry):
@@ -412,9 +456,10 @@
                     sum_hop(step + 1, slot, part, c).wait_send()
     for c in range(CHUNKS):
         stay(c).wait()
-        for step in range(1, GROUPS):
-            ship(step, c, group).wait_send()
-            ship(step, c, lax.rem(group + step, GROUPS)).wait_recv()
+        pass_back(c).wait_send()
+        for step in range(1, 4):
+            ship(step, c, column).wait_send()
+            ship(step, c, lax.rem(column + step, 4)).wait_recv()
     store.wait()
 
 
@@ -449,10 +494,12 @@
             pltpu.VMEM((2, 3, STEP_ROWS, AUX), F32),
             pltpu.VMEM((SLOTS * WIDTH, AUX), F32),
             pltpu.VMEM((SLOTS * WIDTH, AUX), F32),
-            pltpu.VMEM((SLOTS * WIDTH, AUX), F32),
+            pltpu.VMEM((CHUNKS, SLOTS, PART, AUX), F32),
             pltpu.VMEM((OWN, WIDTH, AUX), F32),
             pltpu.VMEM((ALL, 1), F32),
             pltpu.VMEM((4, 1, STACK), F32),
+            pltpu.VMEM((CHUNKS, SLOTS, PART, AUX), F32),
+            pltpu.VMEM((CHUNKS, SLOTS, PART, AUX), F32),
             chunk, chunk, chunk, chunk, chunk, chunk, chunk, chunk,
             dma((GROUPS,)),
             dma((GROUPS,)),
@@ -460,8 +507,8 @@
             dma((BLOCKS,)),
             dma((2 + CHUNKS,)),
             dma((2,)),
-            dma((CHUNKS, GROUPS)),
-            dma((CHUNKS, GROUPS)),
+            dma((CHUNKS, 4)),
+            dma((CHUNKS, 4)),
             dma((SLOTS, CHUNKS)),
             dma((SLOTS, CHUNKS)),
             dma((3, SLOTS, 2, CHUNKS)),
@@ -470,9 +517,13 @@
             dma((3, SLOTS, 2, CHUNKS)),
             dma((SLOTS, CHUNKS)),
             dma((SLOTS, CHUNKS)),
-            dma((CHUNKS, GROUPS)),
-            dma((CHUNKS, GROUPS)),
+            dma((CHUNKS, 4)),
+            dma((CHUNKS, 4)),
             dma((2,)),
+            dma((CHUNKS,)),
+            dma((CHUNKS,)),
+            dma((CHUNKS,)),
+            dma((CHUNKS,)),
         ],
         compiler_params=pltpu.CompilerParams(
             collective_id=0, has_side_effects=True, vmem_limit_bytes=66_000_000),

time: 195 us -> 175 us (0.90)
  Pallas kernels: 194 us -> 174 us
    pallas_call x1, Pallas kernels: 187 us -> 168 us  [run_main(): pl.pallas_call(main_kernel, out_shape=(jax.ShapeDtypeStruct((OWN, WIDTH,...]
where the time goes in v3:
time: 175 us; the launch traced here: 174 us
  Pallas kernels  174 us (99%)
    pallas_call x1, Pallas kernels, run_main(): pl.pallas_call(main_kernel, out_shape=(jax.ShapeDtypeStruct((OWN, WIDTH,...  168 us
    pallas_call x1, Pallas kernels, join(): pl.pallas_call(join_kernel, out_shape=jax.ShapeDtypeStruct((OWN, WIDTH, A...  6.45 us

profile of v3, /device:TPU:0, one launch (start us, length us, event | category | flops | bytes accessed | tf_op | source)
XLA Modules:
  0.0 174.4 jit_solution(15878262966348833177)
XLA Ops:
  0.0 168.0 %main.1 = (f32[12,64,1536]{2,1,0:T(8,128)}, f32[8,64,1536]{2,1,0:T(8,128)}, s32[2,8]{1,0:T(2,128)}) custom-call(s32[1,2]{1,0:T(1,128)} %lists_ref.1, s32[12]{0:T(128)} %orbitals_ref.1, f32[96]{0:T(128)} %occ_ref.1, f32[1,64]{1,0:T(1,128)} %bitcast.1, f32[12,64,1536]{2,1,0:T(8,128)} %held_ref.1), custom_call_target="tpu_custom_call" | custom-call | tf_op jit(solution)/shard_map/main/pallas_call | solution.py:472
  168.0 6.4 %join.1 = f32[12,64,1536]{2,1,0:T(8,128)} custom-call(s32[2,8]{1,0:T(2,128)} %get-tuple-element.8.flags, f32[12,64,1536]{2,1,0:T(8,128)} %get-tuple-element.9.own_ref, f32[8,64,1536]{2,1,0:T(8,128)} %get-tuple-element.10.arrived_ref), custom_call_target="tpu_custom_call" | custom-call | tf_op jit(solution)/shard_map/join/pallas_call | solution.py:544

commit v4 on v3

--- a/solution.py
+++ b/solution.py
@@ -16,18 +16,69 @@
 AUX = 1536
 HELD = OWN * WIDTH
 ALL = 2 * HELD
-CHUNKS = 4
+CHUNKS = 8
+SWAPPED = (3, 5)
 PART = WIDTH // CHUNKS
-HALF = WIDTH // 2
-STEP_ROWS = 2 * SLOTS * HALF
-STACK = 2 * STEP_ROWS
+CALLS = 4
+PIECE = WIDTH // CALLS
+STEP_ROWS = 2 * SLOTS * PIECE
+STACK = 4 * STEP_ROWS
 TILE = 512
 TILES = ALL // TILE
 LANES = 128
 NT = (((1,), (1,)), ((), ()))
 TN = (((0,), (0,)), ((), ()))
-CALL_OF = {(0, 0): (0, 0), (0, 1): (0, 1), (0, 2): (1, 0), (0, 3): (1, 1),
-           (1, 1): (2, 0), (1, 2): (2, 1), (1, 3): (3, 0), (1, 0): (3, 1)}
+OPENING = {
+    0: [("fetch", 0), ("pass", 0), ("fetch", 1), ("hop", 1, 0, 0), ("side", 0, 0), ("fetch", 2),
+        ("hop", 2, 0, 0), ("hop", 1, 1, 0), ("pass", 1), ("hop", 3, 0, 0), ("hop", 2, 1, 0), ("pass", 2),
+        ("fetch", 3), ("hop", 1, 0, 1), ("side", 0, 1), ("hop", 3, 1, 0), ("hop", 1, 0, 2), ("side", 0, 2),
+        ("fetch", 4), ("hop", 2, 0, 1), ("hop", 1, 1, 1), ("pass", 3), ("hop", 2, 0, 2), ("hop", 1, 1, 2),
+        ("pass", 4), ("fetch", 5), ("hop", 3, 0, 1), ("hop", 2, 1, 1), ("side", 0, 3), ("hop", 1, 0, 3),
+        ("hop", 3, 0, 2), ("side", 0, 4), ("fetch", 6), ("hop", 2, 1, 2), ("hop", 1, 0, 4), ("pass", 5),
+        ("hop", 3, 1, 1)],
+    4: [("sum", 2, 6), ("ship", 2), ("sum", 2, 7), ("cross", 4), ("home", 5), ("sum", 3, 6), ("ship", 4),
+        ("sum", 3, 7), ("ship", 5), ("home", 6), ("home", 7), ("cross", 6), ("cross", 7), ("ship", 6),
+        ("ship", 7)],
+}
+BETWEEN = {
+    (0, 0, 0): [("hop", 2, 0, 3), ("fetch", 7), ("side", 1, 3)],
+    (0, 0, 1): [("hop", 3, 1, 2), ("hop", 1, 1, 4)],
+    (0, 0, 2): [("pass", 6), ("hop", 2, 0, 4)],
+    (0, 1, 0): [("hop", 3, 0, 3), ("hop", 1, 0, 5), ("side", 0, 5)],
+    (0, 1, 1): [("hop", 2, 1, 4), ("side", 2, 3)],
+    (0, 1, 2): [("hop", 3, 0, 4), ("hop", 1, 0, 6), ("sum", 1, 0), ("sum", 1, 1)],
+    (0, 2, 0): [("pass", 7), ("hop", 2, 0, 5)],
+    (0, 2, 1): [("hop", 3, 1, 4), ("hop", 2, 0, 6), ("side", 0, 6)],
+    (0, 2, 2): [("side", 3, 3)],
+    (1, 0, 0): [("side", 1, 5), ("sum", 2, 0)],
+    (1, 0, 1): [("sum", 2, 1)],
+    (1, 0, 2): [("hop", 3, 0, 5), ("hop", 1, 0, 7), ("side", 0, 7)],
+    (1, 1, 0): [("hop", 3, 0, 6), ("side", 2, 5)],
+    (1, 1, 1): [("hop", 1, 1, 6)],
+    (1, 1, 2): [("side", 3, 5), ("swap", 0, 3), ("swap", 1, 3), ("swap", 2, 3), ("swap", 3, 3), ("sum", 3, 0),
+        ("sum", 1, 2)],
+    (1, 2, 0): [("sum", 3, 1)],
+    (1, 2, 1): [("hop", 2, 0, 7)],
+    (1, 2, 2): [("hop", 1, 1, 7), ("hop", 2, 1, 6)],
+    (2, 0, 0): [("sum", 1, 3)],
+    (2, 0, 1): [("home", 0)],
+    (2, 0, 2): [("sum", 2, 2)],
+    (2, 1, 0): [("home", 1)],
+    (2, 1, 1): [("hop", 3, 0, 7), ("cross", 0)],
+    (2, 1, 2): [("hop", 2, 1, 7), ("swap", 0, 5), ("swap", 1, 5), ("hop", 3, 1, 6), ("swap", 2, 5),
+        ("swap", 3, 5), ("sum", 1, 4)],
+    (2, 2, 0): [("sum", 2, 3), ("cross", 1)],
+    (2, 2, 1): [("ship", 0), ("sum", 3, 2)],
+    (2, 2, 2): [("hop", 3, 1, 7)],
+    (3, 0, 0): [("sum", 2, 4), ("sum", 1, 5)],
+    (3, 0, 1): [("sum", 3, 3)],
+    (3, 0, 2): [("home", 2)],
+    (3, 1, 1): [("sum", 3, 4)],
+    (3, 1, 2): [("sum", 2, 5), ("sum", 1, 6), ("sum", 1, 7), ("home", 3), ("ship", 1)],
+    (3, 2, 0): [("cross", 2)],
+    (3, 2, 1): [("sum", 3, 5), ("home", 4)],
+    (3, 2, 2): [("ship", 3)],
+}
 
 
 def split(values):
@@ -35,13 +86,8 @@
     return high, (values - high.astype(F32)).astype(BF16)
 
 
-def step_rows(slot, part, c):
-    return pl.ds((slot * 2 + part) * HALF + (c % 2) * PART, PART)
-
-
-def sum_place(step, slot, part, c):
-    call, half = CALL_OF[(c // 2, step)]
-    return call, pl.ds(half * STEP_ROWS + (slot * 2 + part) * HALF + (c % 2) * PART, PART)
+def step_rows(step, slot, part, c):
+    return pl.ds(step * STEP_ROWS + (slot * 2 + part) * PIECE + (c % 2) * PART, PART)
 
 
 def main_kernel(
@@ -50,12 +96,12 @@
     ints_mine, ints_all, vir_mine, vir_all, ints,
     high, low, total, stack, travel, amp, sums, landed,
     side_send, side_land, home, other, row_part, column_part,
-    near_land, near_back,
-    got_0, got_1, got_2, got_3, box_0, box_1, box_2, box_3,
+    near_land, near_back, swapped,
     note_a, note_b, note_c, note_d, local_sem, swap_sem,
     fetch_send, fetch_recv, side_a, side_b,
     hop_send, hop_recv, sum_send, sum_recv, back_a, back_b,
-    out_send, out_recv, own_sem, near_a, near_b, far_a, far_b,
+    out_send, out_recv, own_sem, near_a, near_b, far_a, far_b, trade_a, trade_b,
+    *chunks,
 ):
     group = lax.axis_index("grp")
     block = lax.axis_index("blk")
@@ -73,8 +119,7 @@
         {"blk": side * 8 + lax.rem(level + 1, 4) * 2 + core},
         {"blk": side * 8 + lax.rem(level + 3, 4) * 2 + core},
     )
-    got = (got_0, got_1, got_2, got_3)
-    box = (box_0, box_1, box_2, box_3)
+    got, box = chunks[:CHUNKS], chunks[CHUNKS:]
 
     barrier = pltpu.get_barrier_semaphore()
     for step in range(1, GROUPS):
@@ -93,7 +138,7 @@
     ints_mine[...] = row
     ints_all[group] = row
     vir = vir_ref[...]
-    vir_row = jnp.concatenate([vir[:, :HALF]] * 8 + [vir[:, HALF:]] * 8, axis=1)
+    vir_row = jnp.concatenate([vir, vir], axis=1)
     vir_mine[...] = vir_row
     vir_all[block] = vir_row
     pl.semaphore_wait(barrier, GROUPS + BLOCKS - 2)
@@ -184,43 +229,48 @@
     ]
     for step in range(1, BLOCKS):
         to_block(step, lax.rem(block + step, BLOCKS)).wait_recv()
-    square = (lax.broadcasted_iota(jnp.int32, (HALF, HALF), 0)
-              == lax.broadcasted_iota(jnp.int32, (HALF, HALF), 1))
+    square = (lax.broadcasted_iota(jnp.int32, (WIDTH, WIDTH), 0)
+              == lax.broadcasted_iota(jnp.int32, (WIDTH, WIDTH), 1))
     for owner, place in ((block, 0), (twin_block, 1)):
-        for h in range(2):
-            line = vir_all[owner, :, pl.ds(h * STACK, LANES)][:, :HALF]
-            upright = jnp.sum(jnp.where(square, line, 0.0), axis=1, keepdims=True)
-            for i in range(OWN):
-                energy = occ_ref[ints[group, 0, SLOTS + i]]
-                row_part[pl.ds((place * OWN + i) * WIDTH + h * HALF, HALF), :] = energy - upright
-    piece = lax.broadcasted_iota(jnp.int32, (1, STACK), 1) // HALF
-    for at_call in range(4):
-        terms = jnp.zeros((1, STACK), F32)
-        for (h, step), (call, half) in CALL_OF.items():
-            if call != at_call:
-                continue
-            for slot in range(SLOTS):
-                for part in range(2):
-                    from_level = lax.rem(level + (4 - step if slot == 0 else step), 4)
-                    from_side = side + part - 2 * part * side
-                    line = vir_all[from_side * 8 + from_level * 2 + core, :, pl.ds(h * STACK, STACK)]
-                    here = piece == half * 4 + slot * 2 + part
-                    terms = jnp.where(here, partner_energy[slot] - line, terms)
-        column_part[at_call] = terms
-
-    def beside(slot, c):
-        return remote(stack.at[c // 2, 0, step_rows(slot, 0, c)], stack.at[c // 2, 0, step_rows(slot, 1, c)],
-                      side_a.at[slot, c], side_b.at[slot, c], across)
+        line = vir_all[owner][:, :WIDTH]
+        upright = jnp.sum(jnp.where(square, line, 0.0), axis=1, keepdims=True)
+        for i in range(OWN):
+            energy = occ_ref[ints[group, 0, SLOTS + i]]
+            row_part[pl.ds((place * OWN + i) * WIDTH, WIDTH), :] = energy - upright
+    lines = []
+    for step in range(4):
+        for slot in range(SLOTS):
+            for part in range(2):
+                from_level = lax.rem(level + (4 - step if slot == 0 else step), 4)
+                from_side = side + part - 2 * part * side
+                lines.append(partner_energy[slot] - vir_all[from_side * 8 + from_level * 2 + core])
+    for call in range(CALLS):
+        pieces = [line[:, call * PIECE:(call + 1) * PIECE] for line in lines]
+        column_part[call] = jnp.concatenate(pieces, axis=1)
+
+    def beside(step, slot, c):
+        return remote(stack.at[c // 2, step_rows(step, slot, 0, c)], stack.at[c // 2, step_rows(step, slot, 1, c)],
+                      side_a.at[step, slot, c], side_b.at[step, slot, c], across)
 
     def hop(step, slot, part, c):
-        rows = step_rows(slot, part, c)
-        return remote(stack.at[c // 2, step, rows], stack.at[c // 2, step + 1, rows],
+        return remote(stack.at[c // 2, step_rows(step, slot, part, c)],
+                      stack.at[c // 2, step_rows(step + 1, slot, part, c)],
                       hop_send.at[step, slot, part, c], hop_recv.at[step, slot, part, c], ring[slot])
 
+    def landing(step, slot, part, c):
+        return landed.at[c // 2, step_rows(step - 1, slot, part, c)]
+
     def sum_hop(step, slot, part, c):
-        call, rows = sum_place(step, slot, part, c)
-        return remote(sums.at[call, rows], landed.at[c // 2, step - 1, step_rows(slot, part, c)],
+        return remote(sums.at[c // 2, step_rows(step, slot, part, c)], landing(step, slot, part, c),
                       sum_send.at[step - 1, slot, part, c], sum_recv.at[step - 1, slot, part, c], ring[slot])
+
+    def traded(step, slot, c):
+        return swapped.at[SWAPPED.index(c), step, slot]
+
+    def trade(step, slot, c):
+        place = SWAPPED.index(c)
+        return remote(sums.at[c // 2, step_rows(step, slot, 1, c)], traded(step, slot, c),
+                      trade_a.at[place, step, slot], trade_b.at[place, step, slot], across)
 
     def side_rows(slot, c):
         return pl.ds(slot * WIDTH + c * PART, PART)
@@ -253,47 +303,64 @@
     def on_pass(c):
         pass_on(c).wait_recv()
         for slot in range(SLOTS):
-            stack[c // 2, 0, step_rows(slot, 0, c), :] = (
+            stack[c // 2, step_rows(0, slot, 0, c), :] = (
                 got[c][columns[slot] * 2] * level_with[slot] + near_land[c, slot] * opposed[slot])
         for slot in range(SLOTS):
-            beside(slot, c).start()
+            beside(0, slot, c).start()
             hop(0, slot, 0, c).start()
 
-    def on_side(c):
-        for slot in range(SLOTS):
-            beside(slot, c).wait_recv()
-            hop(0, slot, 1, c).start()
+    def on_side(step, c):
+        for slot in range(SLOTS):
+            beside(step, slot, c).wait_recv()
+            if c not in SWAPPED:
+                hop(0, slot, 1, c).start()
 
     def on_hop(step, part, c):
         for slot in range(SLOTS):
             hop(step - 1, slot, part, c).wait_recv()
             if step < 3:
                 hop(step, slot, part, c).start()
+            if c in SWAPPED:
+                beside(step, slot, c).start()
+
+    def on_swap(step, c):
+        for slot in range(SLOTS):
+            trade(step, slot, c).start()
+
+    def parts_of(c):
+        return (0,) if c in SWAPPED else (1, 0)
 
     def on_sum(step, c):
-        for part in (1, 0):
+        for part in parts_of(c):
             for slot in range(SLOTS):
+                rows = step_rows(step, slot, part, c)
+                if c in SWAPPED:
+                    trade(step, slot, c).wait_recv()
+                    sums[c // 2, rows, :] += traded(step, slot, c)[...]
                 if step > 1:
                     sum_hop(step - 1, slot, part, c).wait_recv()
-                    call, rows = sum_place(step, slot, part, c)
-                    sums[call, rows, :] += landed[c // 2, step - 2, step_rows(slot, part, c), :]
-        for part in (1, 0):
+                    sums[c // 2, rows, :] += landing(step - 1, slot, part, c)[...]
+        for part in parts_of(c):
             for slot in range(SLOTS):
                 sum_hop(step, slot, part, c).start()
 
     def on_home(c):
-        for part in (1, 0):
+        for part in parts_of(c):
             for slot in range(SLOTS):
                 sum_hop(3, slot, part, c).wait_recv()
-                call, rows = sum_place(0, slot, part, c)
-                value = sums[call, rows, :] + landed[c // 2, 2, step_rows(slot, part, c), :]
+                value = sums[c // 2, step_rows(0, slot, part, c), :] + landing(3, slot, part, c)[...]
                 if part:
                     side_send[side_rows(slot, c), :] = value
-                else:
-                    home[c, slot] = value
+                    continue
+                if c in SWAPPED:
+                    trade(0, slot, c).wait_recv()
+                    value += traded(0, slot, c)[...]
+                home[c, slot] = value
             if part:
                 for slot in range(SLOTS):
                     cross(slot, c).start()
+        if c in SWAPPED:
+            pass_back(c).start()
 
     def on_cross(c):
         for slot in range(SLOTS):
@@ -319,73 +386,45 @@
             ship(step, c, column).start()
         stay(c).start()
 
-    def play(*actions):
-        for action, *where in actions:
-            action(*where)
-
-    on_fetch(0)
+    act = {"fetch": on_fetch, "pass": on_pass, "side": on_side, "hop": on_hop, "swap": on_swap,
+           "sum": on_sum, "home": on_home, "cross": on_cross, "ship": on_ship}
+
+    def play(actions):
+        for name, *where in actions:
+            act[name](*where)
+
+    play(OPENING[0][:1])
     swap.wait()
     prepare(total, OWN)
-    play((on_pass, 0), (on_fetch, 1), (on_hop, 1, 0, 0), (on_side, 0), (on_pass, 1), (on_hop, 1, 1, 0),
-         (on_hop, 2, 0, 0), (on_fetch, 2), (on_hop, 1, 0, 1), (on_side, 1), (on_hop, 2, 1, 0), (on_hop, 2, 0, 1),
-         (on_pass, 2), (on_hop, 1, 1, 1))
-
-    open_events = {
-        1: [(on_hop, 3, 0, 0), (on_hop, 3, 1, 0), (on_hop, 3, 0, 1), (on_hop, 3, 1, 1)],
-        3: [(on_hop, 3, 0, 2), (on_hop, 3, 1, 2), (on_hop, 3, 0, 3), (on_hop, 3, 1, 3)],
-    }
-    pair_events = {
-        (0, 0): [(on_fetch, 3)],
-        (0, 1): [(on_hop, 1, 0, 2), (on_side, 2)],
-        (0, 2): [(on_hop, 2, 1, 1)],
-        (1, 1): [(on_hop, 2, 0, 3), (on_hop, 1, 1, 3)],
-        (3, 2): [(on_home, 0)],
-    }
-    back_events = {
-        (0, 1): [(on_hop, 2, 0, 2), (on_pass, 3)],
-        (0, 2): [(on_hop, 1, 1, 2), (on_sum, 1, 0), (on_sum, 1, 1)],
-        (1, 2): [(on_hop, 2, 1, 3), (on_sum, 2, 0), (on_sum, 2, 1)],
-        (2, 0): [(on_sum, 3, 0)],
-        (2, 2): [(on_sum, 3, 1), (on_sum, 1, 2), (on_sum, 1, 3)],
-        (3, 0): [(on_sum, 2, 2)],
-        (3, 1): [(on_home, 1)],
-        (3, 2): [(on_sum, 2, 3)],
-    }
-    own_events = {
-        (0, 1): [(on_hop, 1, 0, 3)],
-        (0, 2): [(on_hop, 2, 1, 2), (on_side, 3)],
-        (3, 0): [(on_cross, 0)],
-        (3, 1): [(on_cross, 1)],
-        (3, 2): [(on_ship, 0)],
-    }
-
-    def run(events, call, index):
-        for (at_call, at_index), actions in events.items():
+    play(OPENING[0][1:])
+
+    def run(call, loop, index):
+        for (at_call, at_loop, at_index), actions in BETWEEN.items():
+            if at_loop != loop:
+                continue
+
             @pl.when((call == at_call) & (index == at_index))
             def _():
-                play(*actions)
+                play(actions)
 
     def one_call(call, carry):
-        for at_call, actions in open_events.items():
-            @pl.when(call == at_call)
-            def _():
-                play(*actions)
-
-        h = call // 2
-        first = (call % 2) * 2 + h
-        second = (first + 1) % 4
+        for at_call in range(1, CALLS):
+            if OPENING.get(at_call):
+                @pl.when(call == at_call)
+                def _():
+                    play(OPENING[at_call])
 
         def cut(index, carry):
-            for half, step in ((0, first), (1, second)):
-                upper, lower = split(stack[h, step, pl.ds(pl.multiple_of(index * 64, 64), 64), :])
-                start = half * STEP_ROWS + index * 64
-                travel[pl.ds(pl.multiple_of(start, 64), 64), :] = upper
-                travel[pl.ds(pl.multiple_of(STACK + start, 64), 64), :] = lower
-                travel[pl.ds(pl.multiple_of(2 * STACK + start, 64), 64), :] = upper
-                sums[call, pl.ds(pl.multiple_of(start, 64), 64), :] = jnp.zeros((64, AUX), F32)
+            start = index * 64
+            rows = pl.ds(pl.multiple_of(start, 64), 64)
+            upper, lower = split(stack[call, rows, :])
+            travel[rows, :] = upper
+            travel[pl.ds(pl.multiple_of(STACK + start, 64), 64), :] = lower
+            travel[pl.ds(pl.multiple_of(2 * STACK + start, 64), 64), :] = upper
+            sums[call, rows, :] = jnp.zeros((64, AUX), F32)
             return carry
 
-        lax.fori_loop(0, STEP_ROWS // 64, cut, 0)
+        lax.fori_loop(0, STACK // 64, cut, 0)
 
         def pair_tile(index, carry):
             rows = pl.ds(pl.multiple_of(index * TILE, TILE), TILE)
@@ -398,7 +437,7 @@
             amp[rows, pl.ds(0, STACK)] = big
             amp[rows, pl.ds(STACK, STACK)] = big
             amp[rows, pl.ds(2 * STACK, STACK)] = small
-            run(pair_events, call, index)
+            run(call, 0, index)
             return carry
 
         lax.fori_loop(0, TILES, pair_tile, 0)
@@ -411,7 +450,7 @@
             back += lax.dot_general(big, low[rows, :], TN, preferred_element_type=F32)
             back += lax.dot_general(amp[rows, pl.ds(2 * STACK, STACK)], upper, TN, preferred_element_type=F32)
             sums[call] += back
-            run(back_events, call, index)
+            run(call, 1, index)
             return carry
 
         lax.fori_loop(0, TILES, back_tile, 0)
@@ -421,18 +460,17 @@
             held = pl.ds(index * (TILE // WIDTH), TILE // WIDTH)
             forward = jnp.dot(amp[rows, :], travel[...], preferred_element_type=F32)
             total[held] += forward.reshape(TILE // WIDTH, WIDTH, AUX)
-            run(own_events, call, index)
+            run(call, 2, index)
             return carry
 
         lax.fori_loop(0, TILES, own_tile, 0)
         return carry
 
-    lax.fori_loop(0, 4, one_call, 0)
+    lax.fori_loop(0, CALLS, one_call, 0)
 
     give = remote(total.at[pl.ds(OWN, OWN)], other, own_sem.at[0], own_sem.at[1], twin)
-    on_sum(3, 2)
     give.start()
-    play((on_sum, 3, 3), (on_ship, 1), (on_home, 2), (on_home, 3), (on_cross, 2), (on_cross, 3), (on_ship, 2), (on_ship, 3))
+    play(OPENING[4])
     give.wait()
 
     def merge(index, carry):
@@ -448,9 +486,13 @@
         to_block(step, block).wait_send()
     for c in range(CHUNKS):
         for slot in range(SLOTS):
-            beside(slot, c).wait_send()
-            cross(slot, c).wait_send()
-            for part in range(2):
+            for step in range(4 if c in SWAPPED else 1):
+                beside(step, slot, c).wait_send()
+                if c in SWAPPED:
+                    trade(step, slot, c).wait_send()
+            if c not in SWAPPED:
+                cross(slot, c).wait_send()
+            for part in parts_of(c):
                 for step in range(3):
                     hop(step, slot, part, c).wait_send()
                     sum_hop(step + 1, slot, part, c).wait_send()
@@ -481,17 +523,17 @@
         scratch_shapes=[
             pltpu.VMEM((1, LANES), jnp.int32),
             pltpu.VMEM((GROUPS, 1, LANES), jnp.int32),
-            pltpu.VMEM((1, 2 * STACK), F32),
-            pltpu.VMEM((BLOCKS, 1, 2 * STACK), F32),
+            pltpu.VMEM((1, LANES), F32),
+            pltpu.VMEM((BLOCKS, 1, LANES), F32),
             pltpu.SMEM((GROUPS, 1, LANES), jnp.int32),
             pltpu.VMEM((ALL, AUX), BF16),
             pltpu.VMEM((ALL, AUX), BF16),
             pltpu.VMEM((2 * OWN, WIDTH, AUX), F32),
-            pltpu.VMEM((2, 4, STEP_ROWS, AUX), F32),
+            pltpu.VMEM((CALLS, STACK, AUX), F32),
             pltpu.VMEM((3 * STACK, AUX), BF16),
             pltpu.VMEM((ALL, 3 * STACK), BF16),
-            pltpu.VMEM((4, STACK, AUX), F32),
-            pltpu.VMEM((2, 3, STEP_ROWS, AUX), F32),
+            pltpu.VMEM((CALLS, STACK, AUX), F32),
+            pltpu.VMEM((CALLS, 3 * STEP_ROWS, AUX), F32),
             pltpu.VMEM((SLOTS * WIDTH, AUX), F32),
             pltpu.VMEM((SLOTS * WIDTH, AUX), F32),
             pltpu.VMEM((CHUNKS, SLOTS, PART, AUX), F32),
@@ -500,7 +542,7 @@
             pltpu.VMEM((4, 1, STACK), F32),
             pltpu.VMEM((CHUNKS, SLOTS, PART, AUX), F32),
             pltpu.VMEM((CHUNKS, SLOTS, PART, AUX), F32),
-            chunk, chunk, chunk, chunk, chunk, chunk, chunk, chunk,
+            pltpu.VMEM((len(SWAPPED), 4, SLOTS, PART, AUX), F32),
             dma((GROUPS,)),
             dma((GROUPS,)),
             dma((BLOCKS,)),
@@ -509,8 +551,8 @@
             dma((2,)),
             dma((CHUNKS, 4)),
             dma((CHUNKS, 4)),
-            dma((SLOTS, CHUNKS)),
-            dma((SLOTS, CHUNKS)),
+            dma((4, SLOTS, CHUNKS)),
+            dma((4, SLOTS, CHUNKS)),
             dma((3, SLOTS, 2, CHUNKS)),
             dma((3, SLOTS, 2, CHUNKS)),
             dma((3, SLOTS, 2, CHUNKS)),
@@ -524,7 +566,9 @@
             dma((CHUNKS,)),
             dma((CHUNKS,)),
             dma((CHUNKS,)),
-        ],
+            dma((len(SWAPPED), 4, SLOTS)),
+            dma((len(SWAPPED), 4, SLOTS)),
+        ] + [chunk] * (2 * CHUNKS),
         compiler_params=pltpu.CompilerParams(
             collective_id=0, has_side_effects=True, vmem_limit_bytes=66_000_000),
         name="main",

time: 175 us -> 158 us (0.903)
  Pallas kernels: 174 us -> 158 us
    pallas_call x1, Pallas kernels: 168 us -> 151 us  [run_main(): pl.pallas_call(main_kernel, out_shape=(jax.ShapeDtypeStruct((OWN, WIDTH,...]
where the time goes in v4:
time: 158 us
  Pallas kernels  158 us (100%)
    pallas_call x1, Pallas kernels, run_main(): pl.pallas_call(main_kernel, out_shape=(jax.ShapeDtypeStruct((OWN, WIDTH,...  151 us
    pallas_call x1, Pallas kernels, join(): pl.pallas_call(join_kernel, out_shape=jax.ShapeDtypeStruct((OWN, WIDTH, A...  6.43 us

profile of v4, /device:TPU:0, one launch (start us, length us, event | category | flops | bytes accessed | tf_op | source)
XLA Modules:
  0.0 157.7 jit_solution(5879809155780551626)
XLA Ops:
  0.0 151.2 %main.1 = (f32[12,64,1536]{2,1,0:T(8,128)}, f32[8,64,1536]{2,1,0:T(8,128)}, s32[2,8]{1,0:T(2,128)}) custom-call(s32[1,2]{1,0:T(1,128)} %lists_ref.1, s32[12]{0:T(128)} %orbitals_ref.1, f32[96]{0:T(128)} %occ_ref.1, f32[1,64]{1,0:T(1,128)} %bitcast.1, f32[12,64,1536]{2,1,0:T(8,128)} %held_ref.1), custom_call_target="tpu_custom_call" | custom-call | tf_op jit(solution)/shard_map/main/pallas_call | solution.py:514
  151.2 6.4 %join.1 = f32[12,64,1536]{2,1,0:T(8,128)} custom-call(s32[2,8]{1,0:T(2,128)} %get-tuple-element.8.flags, f32[12,64,1536]{2,1,0:T(8,128)} %get-tuple-element.9.own_ref, f32[8,64,1536]{2,1,0:T(8,128)} %get-tuple-element.10.arrived_ref), custom_call_target="tpu_custom_call" | custom-call | tf_op jit(solution)/shard_map/join/pallas_call | solution.py:588

commit v5 on v4

--- a/solution.py
+++ b/solution.py
@@ -17,7 +17,8 @@
 HELD = OWN * WIDTH
 ALL = 2 * HELD
 CHUNKS = 8
-SWAPPED = (3, 5)
+SWAPPED = (2, 5)
+HEAD = 8
 PART = WIDTH // CHUNKS
 CALLS = 4
 PIECE = WIDTH // CALLS
@@ -29,55 +30,54 @@
 NT = (((1,), (1,)), ((), ()))
 TN = (((0,), (0,)), ((), ()))
 OPENING = {
-    0: [("fetch", 0), ("pass", 0), ("fetch", 1), ("hop", 1, 0, 0), ("side", 0, 0), ("fetch", 2),
-        ("hop", 2, 0, 0), ("hop", 1, 1, 0), ("pass", 1), ("hop", 3, 0, 0), ("hop", 2, 1, 0), ("pass", 2),
-        ("fetch", 3), ("hop", 1, 0, 1), ("side", 0, 1), ("hop", 3, 1, 0), ("hop", 1, 0, 2), ("side", 0, 2),
-        ("fetch", 4), ("hop", 2, 0, 1), ("hop", 1, 1, 1), ("pass", 3), ("hop", 2, 0, 2), ("hop", 1, 1, 2),
-        ("pass", 4), ("fetch", 5), ("hop", 3, 0, 1), ("hop", 2, 1, 1), ("side", 0, 3), ("hop", 1, 0, 3),
-        ("hop", 3, 0, 2), ("side", 0, 4), ("fetch", 6), ("hop", 2, 1, 2), ("hop", 1, 0, 4), ("pass", 5),
-        ("hop", 3, 1, 1)],
-    4: [("sum", 2, 6), ("ship", 2), ("sum", 2, 7), ("cross", 4), ("home", 5), ("sum", 3, 6), ("ship", 4),
-        ("sum", 3, 7), ("ship", 5), ("home", 6), ("home", 7), ("cross", 6), ("cross", 7), ("ship", 6),
-        ("ship", 7)],
+    0: [("fetch", 0), ("fetch", 1), ("pass", 0), ("hop", 1, 0, 0), ("fetch", 2), ("pass", 1), ("side", 0, 0),
+        ("hop", 2, 0, 0), ("hop", 1, 0, 1), ("fetch", 3), ("pass", 2), ("hop", 1, 1, 0), ("hop", 3, 0, 0),
+        ("side", 0, 1), ("hop", 2, 0, 1), ("hop", 1, 0, 2), ("fetch", 4), ("pass", 3), ("hop", 2, 1, 0),
+        ("hop", 1, 1, 1), ("side", 0, 2), ("hop", 3, 0, 1), ("hop", 2, 0, 2), ("side", 1, 2), ("fetch", 5),
+        ("hop", 1, 0, 3), ("hop", 3, 1, 0), ("pass", 4), ("hop", 2, 1, 1), ("hop", 3, 0, 2), ("side", 0, 3),
+        ("fetch", 6), ("hop", 2, 0, 3), ("hop", 1, 0, 4), ("side", 2, 2), ("hop", 3, 1, 1)],
+    4: [("ship", 1), ("cross", 3), ("sum", 2, 7), ("home", 5), ("cross", 4), ("sum", 3, 6), ("ship", 3),
+        ("sum", 3, 7), ("ship", 5), ("home", 6), ("ship", 4), ("home", 7), ("cross", 6), ("cross", 7),
+        ("ship", 6), ("ship", 7)],
 }
 BETWEEN = {
-    (0, 0, 0): [("hop", 2, 0, 3), ("fetch", 7), ("side", 1, 3)],
-    (0, 0, 1): [("hop", 3, 1, 2), ("hop", 1, 1, 4)],
-    (0, 0, 2): [("pass", 6), ("hop", 2, 0, 4)],
-    (0, 1, 0): [("hop", 3, 0, 3), ("hop", 1, 0, 5), ("side", 0, 5)],
-    (0, 1, 1): [("hop", 2, 1, 4), ("side", 2, 3)],
-    (0, 1, 2): [("hop", 3, 0, 4), ("hop", 1, 0, 6), ("sum", 1, 0), ("sum", 1, 1)],
-    (0, 2, 0): [("pass", 7), ("hop", 2, 0, 5)],
-    (0, 2, 1): [("hop", 3, 1, 4), ("hop", 2, 0, 6), ("side", 0, 6)],
-    (0, 2, 2): [("side", 3, 3)],
-    (1, 0, 0): [("side", 1, 5), ("sum", 2, 0)],
-    (1, 0, 1): [("sum", 2, 1)],
-    (1, 0, 2): [("hop", 3, 0, 5), ("hop", 1, 0, 7), ("side", 0, 7)],
-    (1, 1, 0): [("hop", 3, 0, 6), ("side", 2, 5)],
-    (1, 1, 1): [("hop", 1, 1, 6)],
-    (1, 1, 2): [("side", 3, 5), ("swap", 0, 3), ("swap", 1, 3), ("swap", 2, 3), ("swap", 3, 3), ("sum", 3, 0),
-        ("sum", 1, 2)],
-    (1, 2, 0): [("sum", 3, 1)],
-    (1, 2, 1): [("hop", 2, 0, 7)],
-    (1, 2, 2): [("hop", 1, 1, 7), ("hop", 2, 1, 6)],
-    (2, 0, 0): [("sum", 1, 3)],
-    (2, 0, 1): [("home", 0)],
-    (2, 0, 2): [("sum", 2, 2)],
-    (2, 1, 0): [("home", 1)],
-    (2, 1, 1): [("hop", 3, 0, 7), ("cross", 0)],
-    (2, 1, 2): [("hop", 2, 1, 7), ("swap", 0, 5), ("swap", 1, 5), ("hop", 3, 1, 6), ("swap", 2, 5),
-        ("swap", 3, 5), ("sum", 1, 4)],
-    (2, 2, 0): [("sum", 2, 3), ("cross", 1)],
-    (2, 2, 1): [("ship", 0), ("sum", 3, 2)],
-    (2, 2, 2): [("hop", 3, 1, 7)],
-    (3, 0, 0): [("sum", 2, 4), ("sum", 1, 5)],
+    (0, 0, 0): [("fetch", 7), ("hop", 1, 1, 3), ("pass", 5), ("hop", 3, 0, 3)],
+    (0, 0, 1): [("side", 0, 4), ("hop", 2, 0, 4)],
+    (0, 0, 2): [("side", 3, 2), ("hop", 2, 1, 3)],
+    (0, 1, 0): [("hop", 1, 0, 5)],
+    (0, 1, 1): [("pass", 6), ("hop", 1, 1, 4), ("hop", 3, 0, 4)],
+    (0, 1, 2): [("hop", 3, 1, 3), ("sum", 1, 0), ("sum", 1, 1)],
+    (0, 2, 0): [("pass", 7), ("side", 0, 5), ("hop", 2, 0, 5), ("hop", 1, 0, 6)],
+    (0, 2, 1): [("hop", 2, 1, 4)],
+    (0, 2, 2): [("side", 1, 5)],
+    (1, 0, 0): [("side", 0, 6)],
+    (1, 0, 1): [("side", 0, 7), ("hop", 1, 0, 7)],
+    (1, 0, 2): [("side", 2, 5), ("hop", 3, 0, 5), ("hop", 2, 0, 6)],
+    (1, 1, 0): [("hop", 3, 1, 4), ("sum", 2, 0)],
+    (1, 1, 1): [("hop", 1, 1, 6), ("hop", 1, 1, 7)],
+    (1, 1, 2): [("side", 3, 5), ("hop", 2, 0, 7), ("swap", 0, 2), ("swap", 1, 2), ("swap", 2, 2), ("swap", 3, 2)],
+    (1, 2, 0): [("hop", 3, 0, 6), ("sum", 2, 1)],
+    (1, 2, 1): [("sum", 3, 0)],
+    (1, 2, 2): [("hop", 2, 1, 6), ("hop", 2, 1, 7)],
+    (2, 0, 0): [("hop", 3, 0, 7)],
+    (2, 0, 1): [("sum", 3, 1)],
+    (2, 0, 2): [("home", 0), ("sum", 1, 2)],
+    (2, 1, 0): [("hop", 3, 1, 6), ("sum", 1, 3)],
+    (2, 1, 1): [("hop", 3, 1, 7)],
+    (2, 1, 2): [("swap", 0, 5), ("swap", 1, 5), ("swap", 2, 5), ("swap", 3, 5), ("cross", 0), ("home", 1),
+        ("sum", 1, 4)],
+    (2, 2, 0): [("sum", 2, 2)],
+    (2, 2, 1): [("sum", 2, 3)],
+    (2, 2, 2): [("sum", 2, 4)],
+    (3, 0, 0): [("sum", 3, 2), ("sum", 1, 5)],
     (3, 0, 1): [("sum", 3, 3)],
-    (3, 0, 2): [("home", 2)],
-    (3, 1, 1): [("sum", 3, 4)],
-    (3, 1, 2): [("sum", 2, 5), ("sum", 1, 6), ("sum", 1, 7), ("home", 3), ("ship", 1)],
-    (3, 2, 0): [("cross", 2)],
-    (3, 2, 1): [("sum", 3, 5), ("home", 4)],
-    (3, 2, 2): [("ship", 3)],
+    (3, 0, 2): [("sum", 3, 4)],
+    (3, 1, 0): [("home", 2)],
+    (3, 1, 1): [("sum", 2, 5)],
+    (3, 1, 2): [("ship", 0), ("cross", 1), ("home", 3), ("sum", 1, 6), ("sum", 1, 7)],
+    (3, 2, 0): [("home", 4)],
+    (3, 2, 1): [("ship", 2), ("sum", 3, 5)],
+    (3, 2, 2): [("sum", 2, 6)],
 }
 
 
@@ -97,10 +97,8 @@
     high, low, total, stack, travel, amp, sums, landed,
     side_send, side_land, home, other, row_part, column_part,
     near_land, near_back, swapped,
-    note_a, note_b, note_c, note_d, local_sem, swap_sem,
-    fetch_send, fetch_recv, side_a, side_b,
-    hop_send, hop_recv, sum_send, sum_recv, back_a, back_b,
-    out_send, out_recv, own_sem, near_a, near_b, far_a, far_b, trade_a, trade_b,
+    note_sem, sent_sem, local_sem, swap_sem, box_sem, fetch_recv, side_recv, side_more,
+    hop_recv, sum_recv, cross_recv, out_recv, own_sem, near_recv, far_recv, trade_recv,
     *chunks,
 ):
     group = lax.axis_index("grp")
@@ -146,12 +144,21 @@
     def remote(src, dst, send, recv, peer):
         return pltpu.make_async_remote_copy(src, dst, send, recv, device_id=peer, device_id_type=MESH)
 
+    def drain(like, sem):
+        pltpu.make_async_copy(like, like, sem).wait()
+
+    def drain_rows(count, sem):
+        if count < WIDTH:
+            drain(total.at[0, pl.ds(0, count)], sem)
+        else:
+            drain(total.at[pl.ds(0, count // WIDTH)], sem)
+
     def to_group(step, slot):
-        return remote(ints_mine, ints_all.at[slot], note_a.at[step], note_b.at[slot],
+        return remote(ints_mine, ints_all.at[slot], note_sem.at[0], note_sem.at[1],
                       {"grp": lax.rem(group + step, GROUPS)})
 
     def to_block(step, slot):
-        return remote(vir_mine, vir_all.at[slot], note_c.at[step], note_d.at[slot],
+        return remote(vir_mine, vir_all.at[slot], note_sem.at[2], note_sem.at[3],
                       {"blk": lax.rem(block + step, BLOCKS)})
 
     for step in range(1, GROUPS):
@@ -159,8 +166,8 @@
     for step in range(1, BLOCKS):
         to_block(step, block).start()
     keep.wait()
-    for step in range(1, GROUPS):
-        to_group(step, lax.rem(group + step, GROUPS)).wait_recv()
+    few, most = ints_all.at[pl.ds(0, GROUPS - 1)], vir_all.at[pl.ds(0, BLOCKS - 1)]
+    drain(few, note_sem.at[1])
     to_scalar = pltpu.make_async_copy(ints_all, ints, local_sem.at[1])
     to_scalar.start()
     to_scalar.wait()
@@ -183,7 +190,7 @@
 
     def fetch(step, c, x):
         return remote(box[c].at[pl.ds(step * 2, 2)], got[c].at[pl.ds(x * 2, 2)],
-                      fetch_send.at[c, step], fetch_recv.at[c, x], {"grp": held_by(step, 0)})
+                      box_sem.at[c], fetch_recv.at[c], {"grp": held_by(step, 0)})
 
     def fill(c):
         for step in range(4):
@@ -227,8 +234,7 @@
     partner_energy = [
         occ_ref[ints[sources[slot], 0, SLOTS + mine[slot] % OWN]] for slot in range(SLOTS)
     ]
-    for step in range(1, BLOCKS):
-        to_block(step, lax.rem(block + step, BLOCKS)).wait_recv()
+    drain(most, note_sem.at[3])
     square = (lax.broadcasted_iota(jnp.int32, (WIDTH, WIDTH), 0)
               == lax.broadcasted_iota(jnp.int32, (WIDTH, WIDTH), 1))
     for owner, place in ((block, 0), (twin_block, 1)):
@@ -248,21 +254,25 @@
         pieces = [line[:, call * PIECE:(call + 1) * PIECE] for line in lines]
         column_part[call] = jnp.concatenate(pieces, axis=1)
 
+    def side_came(step, c):
+        return side_more.at[SWAPPED.index(c), step - 1] if step else side_recv.at[c]
+
     def beside(step, slot, c):
+        came = side_came(step, c)
         return remote(stack.at[c // 2, step_rows(step, slot, 0, c)], stack.at[c // 2, step_rows(step, slot, 1, c)],
-                      side_a.at[step, slot, c], side_b.at[step, slot, c], across)
+                      sent_sem.at[1], came, across)
 
     def hop(step, slot, part, c):
         return remote(stack.at[c // 2, step_rows(step, slot, part, c)],
                       stack.at[c // 2, step_rows(step + 1, slot, part, c)],
-                      hop_send.at[step, slot, part, c], hop_recv.at[step, slot, part, c], ring[slot])
+                      sent_sem.at[0], hop_recv.at[step, part, c], ring[slot])
 
     def landing(step, slot, part, c):
         return landed.at[c // 2, step_rows(step - 1, slot, part, c)]
 
     def sum_hop(step, slot, part, c):
         return remote(sums.at[c // 2, step_rows(step, slot, part, c)], landing(step, slot, part, c),
-                      sum_send.at[step - 1, slot, part, c], sum_recv.at[step - 1, slot, part, c], ring[slot])
+                      sent_sem.at[0], sum_recv.at[step - 1, part, c], ring[slot])
 
     def traded(step, slot, c):
         return swapped.at[SWAPPED.index(c), step, slot]
@@ -270,32 +280,31 @@
     def trade(step, slot, c):
         place = SWAPPED.index(c)
         return remote(sums.at[c // 2, step_rows(step, slot, 1, c)], traded(step, slot, c),
-                      trade_a.at[place, step, slot], trade_b.at[place, step, slot], across)
+                      sent_sem.at[1], trade_recv.at[place, step], across)
 
     def side_rows(slot, c):
         return pl.ds(slot * WIDTH + c * PART, PART)
 
     def cross(slot, c):
         rows = side_rows(slot, c)
-        return remote(side_send.at[rows], side_land.at[rows], back_a.at[slot, c], back_b.at[slot, c], across)
+        return remote(side_send.at[rows], side_land.at[rows], sent_sem.at[1], cross_recv.at[c], across)
 
     def pass_on(c):
-        return remote(box[c].at[pl.ds(0, 2)], near_land.at[c], near_a.at[c], near_b.at[c], facing)
+        return remote(box[c].at[pl.ds(0, 2)], near_land.at[c], box_sem.at[c], near_recv.at[c], facing)
 
     def pass_back(c):
-        return remote(home.at[c], near_back.at[c], far_a.at[c], far_b.at[c], facing)
+        return remote(home.at[c], near_back.at[c], sent_sem.at[1], far_recv.at[c], facing)
 
     def ship(step, c, x):
         return remote(box[c].at[pl.ds(step * 2, 2)], arrived.at[pl.ds(x * 2, 2), pl.ds(c * PART, PART)],
-                      out_send.at[c, step], out_recv.at[c, x], {"grp": held_by(step, 0)})
+                      sent_sem.at[1], out_recv.at[0], {"grp": held_by(step, 0)})
 
     def stay(c):
         return pltpu.make_async_copy(
             box[c].at[pl.ds(0, 2)], arrived.at[pl.ds(column * 2, 2), pl.ds(c * PART, PART)], local_sem.at[2 + c])
 
     def on_fetch(c):
-        for step in range(1, 4):
-            fetch(step, c, lax.rem(column + step, 4)).wait_recv()
+        drain_rows(6 * PART, fetch_recv.at[c])
         for slot in range(SLOTS):
             box[c][slot] = got[c][their_columns[slot] * 2 + 1]
         pass_on(c).start()
@@ -310,14 +319,14 @@
             hop(0, slot, 0, c).start()
 
     def on_side(step, c):
+        drain_rows(2 * PART, side_came(step, c))
+        if c not in SWAPPED:
+            for slot in range(SLOTS):
+                hop(0, slot, 1, c).start()
+
+    def on_hop(step, part, c):
+        drain_rows(2 * PART, hop_recv.at[step - 1, part, c])
         for slot in range(SLOTS):
-            beside(step, slot, c).wait_recv()
-            if c not in SWAPPED:
-                hop(0, slot, 1, c).start()
-
-    def on_hop(step, part, c):
-        for slot in range(SLOTS):
-            hop(step - 1, slot, part, c).wait_recv()
             if step < 3:
                 hop(step, slot, part, c).start()
             if c in SWAPPED:
@@ -331,29 +340,32 @@
         return (0,) if c in SWAPPED else (1, 0)
 
     def on_sum(step, c):
+        if c in SWAPPED:
+            drain_rows(2 * PART, trade_recv.at[SWAPPED.index(c), step])
         for part in parts_of(c):
+            if step > 1:
+                drain_rows(2 * PART, sum_recv.at[step - 2, part, c])
             for slot in range(SLOTS):
                 rows = step_rows(step, slot, part, c)
                 if c in SWAPPED:
-                    trade(step, slot, c).wait_recv()
                     sums[c // 2, rows, :] += traded(step, slot, c)[...]
                 if step > 1:
-                    sum_hop(step - 1, slot, part, c).wait_recv()
                     sums[c // 2, rows, :] += landing(step - 1, slot, part, c)[...]
         for part in parts_of(c):
             for slot in range(SLOTS):
                 sum_hop(step, slot, part, c).start()
 
     def on_home(c):
+        if c in SWAPPED:
+            drain_rows(2 * PART, trade_recv.at[SWAPPED.index(c), 0])
         for part in parts_of(c):
+            drain_rows(2 * PART, sum_recv.at[2, part, c])
             for slot in range(SLOTS):
-                sum_hop(3, slot, part, c).wait_recv()
                 value = sums[c // 2, step_rows(0, slot, part, c), :] + landing(3, slot, part, c)[...]
                 if part:
                     side_send[side_rows(slot, c), :] = value
                     continue
                 if c in SWAPPED:
-                    trade(0, slot, c).wait_recv()
                     value += traded(0, slot, c)[...]
                 home[c, slot] = value
             if part:
@@ -363,15 +375,13 @@
             pass_back(c).start()
 
     def on_cross(c):
+        drain_rows(2 * PART, cross_recv.at[c])
         for slot in range(SLOTS):
-            cross(slot, c).wait_recv()
             home[c, slot] += side_land[side_rows(slot, c), :]
         pass_back(c).start()
 
     def on_ship(c):
-        for step in range(1, 4):
-            fetch(step, c, column).wait_send()
-        pass_on(c).wait_send()
+        drain_rows(8 * PART, box_sem.at[c])
 
         def blend(rows, source, step):
             picks = [jnp.where(row // OWN == held_by(step, 0), one, none) for row in rows]
@@ -393,10 +403,10 @@
         for name, *where in actions:
             act[name](*where)
 
-    play(OPENING[0][:1])
+    play(OPENING[0][:HEAD])
     swap.wait()
     prepare(total, OWN)
-    play(OPENING[0][1:])
+    play(OPENING[0][HEAD:])
 
     def run(call, loop, index):
         for (at_call, at_loop, at_index), actions in BETWEEN.items():
@@ -480,28 +490,16 @@
     lax.fori_loop(0, OWN, merge, 0)
     store = pltpu.make_async_copy(total.at[pl.ds(0, OWN)], own_out, local_sem.at[0])
     store.start()
-    for step in range(1, GROUPS):
-        to_group(step, group).wait_send()
-    for step in range(1, BLOCKS):
-        to_block(step, block).wait_send()
-    for c in range(CHUNKS):
-        for slot in range(SLOTS):
-            for step in range(4 if c in SWAPPED else 1):
-                beside(step, slot, c).wait_send()
-                if c in SWAPPED:
-                    trade(step, slot, c).wait_send()
-            if c not in SWAPPED:
-                cross(slot, c).wait_send()
-            for part in parts_of(c):
-                for step in range(3):
-                    hop(step, slot, part, c).wait_send()
-                    sum_hop(step + 1, slot, part, c).wait_send()
+    swaps = len(SWAPPED)
+    ring_rows = 2 * 3 * SLOTS * PART * (2 * CHUNKS - swaps)
+    other_rows = SLOTS * PART * (CHUNKS + 7 * swaps + (CHUNKS - swaps) + CHUNKS + 3 * CHUNKS)
     for c in range(CHUNKS):
         stay(c).wait()
-        pass_back(c).wait_send()
-        for step in range(1, 4):
-            ship(step, c, column).wait_send()
-            ship(step, c, lax.rem(column + step, 4)).wait_recv()
+    drain(few, note_sem.at[0])
+    drain(most, note_sem.at[2])
+    drain_rows(ring_rows, sent_sem.at[0])
+    drain_rows(other_rows, sent_sem.at[1])
+    drain_rows(3 * SLOTS * WIDTH, out_recv.at[0])
     store.wait()
 
 
@@ -543,31 +541,22 @@
             pltpu.VMEM((CHUNKS, SLOTS, PART, AUX), F32),
             pltpu.VMEM((CHUNKS, SLOTS, PART, AUX), F32),
             pltpu.VMEM((len(SWAPPED), 4, SLOTS, PART, AUX), F32),
-            dma((GROUPS,)),
-            dma((GROUPS,)),
-            dma((BLOCKS,)),
-            dma((BLOCKS,)),
+            dma((4,)),
+            dma((2,)),
             dma((2 + CHUNKS,)),
-            dma((2,)),
-            dma((CHUNKS, 4)),
-            dma((CHUNKS, 4)),
-            dma((4, SLOTS, CHUNKS)),
-            dma((4, SLOTS, CHUNKS)),
-            dma((3, SLOTS, 2, CHUNKS)),
-            dma((3, SLOTS, 2, CHUNKS)),
-            dma((3, SLOTS, 2, CHUNKS)),
-            dma((3, SLOTS, 2, CHUNKS)),
-            dma((SLOTS, CHUNKS)),
-            dma((SLOTS, CHUNKS)),
-            dma((CHUNKS, 4)),
-            dma((CHUNKS, 4)),
             dma((2,)),
             dma((CHUNKS,)),
             dma((CHUNKS,)),
             dma((CHUNKS,)),
+            dma((len(SWAPPED), 3)),
+            dma((3, 2, CHUNKS)),
+            dma((3, 2, CHUNKS)),
             dma((CHUNKS,)),
-            dma((len(SWAPPED), 4, SLOTS)),
-            dma((len(SWAPPED), 4, SLOTS)),
+            dma((1,)),
+            dma((2,)),
+            dma((CHUNKS,)),
+            dma((CHUNKS,)),
+            dma((len(SWAPPED), 4)),
         ] + [chunk] * (2 * CHUNKS),
         compiler_params=pltpu.CompilerParams(
             collective_id=0, has_side_effects=True, vmem_limit_bytes=66_000_000),

time: 158 us -> 149 us (0.943)
  Pallas kernels: 158 us -> 149 us
    pallas_call x1, Pallas kernels: 151 us -> 142 us  [run_main(): pl.pallas_call(main_kernel, out_shape=(jax.ShapeDtypeStruct((OWN, WIDTH,...]
where the time goes in v5:
time: 149 us
  Pallas kernels  149 us (100%)
    pallas_call x1, Pallas kernels, run_main(): pl.pallas_call(main_kernel, out_shape=(jax.ShapeDtypeStruct((OWN, WIDTH,...  142 us
    pallas_call x1, Pallas kernels, join(): pl.pallas_call(join_kernel, out_shape=jax.ShapeDtypeStruct((OWN, WIDTH, A...  6.47 us

profile of v5, /device:TPU:0, one launch (start us, length us, event | category | flops | bytes accessed | tf_op | source)
XLA Modules:
  0.0 148.7 jit_solution(10658648378030942406)
XLA Ops:
  0.0 142.2 %main.1 = (f32[12,64,1536]{2,1,0:T(8,128)}, f32[8,64,1536]{2,1,0:T(8,128)}, s32[2,8]{1,0:T(2,128)}) custom-call(s32[1,2]{1,0:T(1,128)} %lists_ref.1, s32[12]{0:T(128)} %orbitals_ref.1, f32[96]{0:T(128)} %occ_ref.1, f32[1,64]{1,0:T(1,128)} %bitcast.1, f32[12,64,1536]{2,1,0:T(8,128)} %held_ref.1), custom_call_target="tpu_custom_call" | custom-call | tf_op jit(solution)/shard_map/main/pallas_call | solution.py:512
  142.2 6.5 %join.1 = f32[12,64,1536]{2,1,0:T(8,128)} custom-call(s32[2,8]{1,0:T(2,128)} %get-tuple-element.8.flags, f32[12,64,1536]{2,1,0:T(8,128)} %get-tuple-element.9.own_ref, f32[8,64,1536]{2,1,0:T(8,128)} %get-tuple-element.10.arrived_ref), custom_call_target="tpu_custom_call" | custom-call | tf_op jit(solution)/shard_map/join/pallas_call | solution.py:577

commit v6 on v5

--- a/solution.py
+++ b/solution.py
@@ -30,54 +30,51 @@
 NT = (((1,), (1,)), ((), ()))
 TN = (((0,), (0,)), ((), ()))
 OPENING = {
-    0: [("fetch", 0), ("fetch", 1), ("pass", 0), ("hop", 1, 0, 0), ("fetch", 2), ("pass", 1), ("side", 0, 0),
-        ("hop", 2, 0, 0), ("hop", 1, 0, 1), ("fetch", 3), ("pass", 2), ("hop", 1, 1, 0), ("hop", 3, 0, 0),
-        ("side", 0, 1), ("hop", 2, 0, 1), ("hop", 1, 0, 2), ("fetch", 4), ("pass", 3), ("hop", 2, 1, 0),
-        ("hop", 1, 1, 1), ("side", 0, 2), ("hop", 3, 0, 1), ("hop", 2, 0, 2), ("side", 1, 2), ("fetch", 5),
-        ("hop", 1, 0, 3), ("hop", 3, 1, 0), ("pass", 4), ("hop", 2, 1, 1), ("hop", 3, 0, 2), ("side", 0, 3),
-        ("fetch", 6), ("hop", 2, 0, 3), ("hop", 1, 0, 4), ("side", 2, 2), ("hop", 3, 1, 1)],
-    4: [("ship", 1), ("cross", 3), ("sum", 2, 7), ("home", 5), ("cross", 4), ("sum", 3, 6), ("ship", 3),
-        ("sum", 3, 7), ("ship", 5), ("home", 6), ("ship", 4), ("home", 7), ("cross", 6), ("cross", 7),
-        ("ship", 6), ("ship", 7)],
+    0: [("fetch", 0), ("fetch", 1), ("pass", 0), ("hop", 1, 0, 0), ("fetch", 2), ("hop", 3, 0, 0), ("pass", 1),
+        ("side", 0, 0), ("hop", 2, 0, 0), ("hop", 1, 0, 1), ("fetch", 3), ("pass", 2), ("hop", 3, 0, 1),
+        ("hop", 1, 1, 0), ("side", 0, 1), ("hop", 3, 1, 0), ("hop", 2, 0, 1), ("fetch", 4), ("pass", 3),
+        ("hop", 3, 0, 2), ("side", 0, 2), ("hop", 2, 1, 0), ("hop", 1, 0, 2), ("hop", 1, 1, 1), ("fetch", 5),
+        ("hop", 3, 1, 1), ("pass", 4), ("hop", 3, 0, 3), ("side", 0, 3), ("hop", 2, 0, 2), ("side", 3, 2),
+        ("fetch", 6), ("hop", 2, 1, 1)],
+    4: [("sum", 3, 6), ("ship", 1), ("cross", 4), ("sum", 1, 7), ("home", 5), ("ship", 3), ("sum", 3, 7),
+        ("ship", 4), ("home", 6), ("ship", 5), ("cross", 6), ("home", 7), ("ship", 6), ("cross", 7), ("ship", 7)],
 }
 BETWEEN = {
-    (0, 0, 0): [("fetch", 7), ("hop", 1, 1, 3), ("pass", 5), ("hop", 3, 0, 3)],
-    (0, 0, 1): [("side", 0, 4), ("hop", 2, 0, 4)],
-    (0, 0, 2): [("side", 3, 2), ("hop", 2, 1, 3)],
-    (0, 1, 0): [("hop", 1, 0, 5)],
-    (0, 1, 1): [("pass", 6), ("hop", 1, 1, 4), ("hop", 3, 0, 4)],
-    (0, 1, 2): [("hop", 3, 1, 3), ("sum", 1, 0), ("sum", 1, 1)],
-    (0, 2, 0): [("pass", 7), ("side", 0, 5), ("hop", 2, 0, 5), ("hop", 1, 0, 6)],
-    (0, 2, 1): [("hop", 2, 1, 4)],
-    (0, 2, 2): [("side", 1, 5)],
-    (1, 0, 0): [("side", 0, 6)],
-    (1, 0, 1): [("side", 0, 7), ("hop", 1, 0, 7)],
-    (1, 0, 2): [("side", 2, 5), ("hop", 3, 0, 5), ("hop", 2, 0, 6)],
-    (1, 1, 0): [("hop", 3, 1, 4), ("sum", 2, 0)],
-    (1, 1, 1): [("hop", 1, 1, 6), ("hop", 1, 1, 7)],
-    (1, 1, 2): [("side", 3, 5), ("hop", 2, 0, 7), ("swap", 0, 2), ("swap", 1, 2), ("swap", 2, 2), ("swap", 3, 2)],
-    (1, 2, 0): [("hop", 3, 0, 6), ("sum", 2, 1)],
-    (1, 2, 1): [("sum", 3, 0)],
-    (1, 2, 2): [("hop", 2, 1, 6), ("hop", 2, 1, 7)],
-    (2, 0, 0): [("hop", 3, 0, 7)],
-    (2, 0, 1): [("sum", 3, 1)],
-    (2, 0, 2): [("home", 0), ("sum", 1, 2)],
-    (2, 1, 0): [("hop", 3, 1, 6), ("sum", 1, 3)],
-    (2, 1, 1): [("hop", 3, 1, 7)],
-    (2, 1, 2): [("swap", 0, 5), ("swap", 1, 5), ("swap", 2, 5), ("swap", 3, 5), ("cross", 0), ("home", 1),
-        ("sum", 1, 4)],
-    (2, 2, 0): [("sum", 2, 2)],
-    (2, 2, 1): [("sum", 2, 3)],
-    (2, 2, 2): [("sum", 2, 4)],
-    (3, 0, 0): [("sum", 3, 2), ("sum", 1, 5)],
-    (3, 0, 1): [("sum", 3, 3)],
+    (0, 0, 0): [("side", 1, 2), ("hop", 1, 0, 3), ("hop", 1, 0, 4), ("hop", 3, 0, 4)],
+    (0, 0, 1): [("fetch", 7), ("hop", 1, 1, 3)],
+    (0, 0, 2): [("pass", 5), ("hop", 2, 0, 3), ("hop", 3, 1, 3), ("side", 0, 4)],
+    (0, 1, 0): [("hop", 2, 0, 4)],
+    (0, 1, 1): [("side", 2, 2), ("hop", 2, 1, 3), ("hop", 1, 0, 5)],
+    (0, 1, 2): [("hop", 3, 0, 5), ("sum", 2, 0), ("sum", 1, 0)],
+    (0, 2, 0): [("hop", 1, 1, 4), ("hop", 3, 1, 4)],
+    (0, 2, 1): [("hop", 2, 0, 5), ("sum", 2, 1)],
+    (0, 2, 2): [("side", 0, 5)],
+    (1, 0, 0): [("pass", 6), ("side", 1, 5)],
+    (1, 0, 1): [("pass", 7), ("hop", 2, 1, 4), ("side", 3, 5)],
+    (1, 0, 2): [("side", 2, 5), ("sum", 3, 0)],
+    (1, 1, 0): [("hop", 1, 0, 6)],
+    (1, 1, 1): [("side", 0, 6), ("hop", 3, 0, 6), ("hop", 1, 0, 7)],
+    (1, 1, 2): [("side", 0, 7), ("hop", 3, 0, 7), ("swap", 0, 2), ("swap", 1, 2), ("swap", 2, 2), ("swap", 3, 2)],
+    (1, 2, 0): [("home", 0)],
+    (1, 2, 1): [("hop", 2, 0, 6), ("sum", 3, 1)],
+    (1, 2, 2): [("hop", 1, 1, 6), ("hop", 3, 1, 6)],
+    (2, 0, 0): [("hop", 1, 1, 7), ("hop", 2, 0, 7)],
+    (2, 0, 1): [("hop", 3, 1, 7), ("sum", 1, 1)],
+    (2, 0, 2): [("sum", 2, 2), ("sum", 1, 2)],
+    (2, 1, 0): [("hop", 2, 1, 6), ("sum", 2, 3)],
+    (2, 1, 1): [("hop", 2, 1, 7), ("cross", 0)],
+    (2, 1, 2): [("swap", 0, 5), ("swap", 1, 5), ("swap", 2, 5), ("swap", 3, 5), ("home", 1), ("sum", 1, 3)],
+    (2, 2, 0): [("sum", 3, 2)],
+    (2, 2, 1): [("sum", 2, 4)],
+    (2, 2, 2): [("ship", 0), ("sum", 3, 3)],
+    (3, 0, 0): [("home", 2), ("sum", 1, 4)],
+    (3, 0, 1): [("sum", 1, 5)],
     (3, 0, 2): [("sum", 3, 4)],
-    (3, 1, 0): [("home", 2)],
-    (3, 1, 1): [("sum", 2, 5)],
-    (3, 1, 2): [("ship", 0), ("cross", 1), ("home", 3), ("sum", 1, 6), ("sum", 1, 7)],
-    (3, 2, 0): [("home", 4)],
-    (3, 2, 1): [("ship", 2), ("sum", 3, 5)],
-    (3, 2, 2): [("sum", 2, 6)],
+    (3, 1, 0): [("home", 3), ("sum", 2, 5)],
+    (3, 1, 1): [("cross", 1)],
+    (3, 1, 2): [("sum", 2, 6), ("sum", 1, 6)],
+    (3, 2, 0): [("ship", 2), ("home", 4)],
+    (3, 2, 1): [("cross", 3), ("sum", 3, 5), ("sum", 2, 7)],
 }
 
 
@@ -98,7 +95,7 @@
     side_send, side_land, home, other, row_part, column_part,
     near_land, near_back, swapped,
     note_sem, sent_sem, local_sem, swap_sem, box_sem, fetch_recv, side_recv, side_more,
-    hop_recv, sum_recv, cross_recv, out_recv, own_sem, near_recv, far_recv, trade_recv,
+    hop_recv, sum_recv, cross_recv, out_recv, own_sem, near_recv, far_recv, trade_recv, clear_sem,
     *chunks,
 ):
     group = lax.axis_index("grp")
@@ -144,6 +141,8 @@
     def remote(src, dst, send, recv, peer):
         return pltpu.make_async_remote_copy(src, dst, send, recv, device_id=peer, device_id_type=MESH)
 
+    swap = remote(held_ref, total.at[pl.ds(OWN, OWN)], swap_sem.at[0], swap_sem.at[1], twin)
+
     def drain(like, sem):
         pltpu.make_async_copy(like, like, sem).wait()
 
@@ -165,6 +164,7 @@
         to_group(step, group).start()
     for step in range(1, BLOCKS):
         to_block(step, block).start()
+    swap.start()
     keep.wait()
     few, most = ints_all.at[pl.ds(0, GROUPS - 1)], vir_all.at[pl.ds(0, BLOCKS - 1)]
     drain(few, note_sem.at[1])
@@ -208,8 +208,6 @@
         for step in range(1, 4):
             fetch(step, c, column).start()
 
-    swap = remote(held_ref, total.at[pl.ds(OWN, OWN)], swap_sem.at[0], swap_sem.at[1], twin)
-
     def prepare(source, first):
         def tile(index, carry):
             rows = pl.ds(pl.multiple_of((first + index) * WIDTH, WIDTH), WIDTH)
@@ -221,7 +219,7 @@
         lax.fori_loop(0, OWN, tile, 0)
 
     prepare(other, 0)
-    swap.start()
+    pl.semaphore_signal(clear_sem, 1, device_id=twin, device_id_type=MESH)
 
     mine = [ints[group, 0, slot] for slot in range(SLOTS)]
     theirs = [ints[opposite, 0, slot] for slot in range(SLOTS)]
@@ -263,16 +261,17 @@
                       sent_sem.at[1], came, across)
 
     def hop(step, slot, part, c):
-        return remote(stack.at[c // 2, step_rows(step, slot, part, c)],
-                      stack.at[c // 2, step_rows(step + 1, slot, part, c)],
-                      sent_sem.at[0], hop_recv.at[step, part, c], ring[slot])
+        source = 1 if step == 2 else 0
+        return remote(stack.at[c // 2, step_rows(source, slot, part, c)],
+                      stack.at[c // 2, step_rows(step, slot, part, c)],
+                      sent_sem.at[0], hop_recv.at[step - 1, part, c], ring[1 - slot if step == 3 else slot])
 
     def landing(step, slot, part, c):
         return landed.at[c // 2, step_rows(step - 1, slot, part, c)]
 
     def sum_hop(step, slot, part, c):
         return remote(sums.at[c // 2, step_rows(step, slot, part, c)], landing(step, slot, part, c),
-                      sent_sem.at[0], sum_recv.at[step - 1, part, c], ring[slot])
+                      sent_sem.at[0], sum_recv.at[step - 1, part, c], ring[1 - slot if step == 1 else slot])
 
     def traded(step, slot, c):
         return swapped.at[SWAPPED.index(c), step, slot]
@@ -316,19 +315,21 @@
                 got[c][columns[slot] * 2] * level_with[slot] + near_land[c, slot] * opposed[slot])
         for slot in range(SLOTS):
             beside(0, slot, c).start()
-            hop(0, slot, 0, c).start()
+            hop(1, slot, 0, c).start()
+            hop(3, slot, 0, c).start()
 
     def on_side(step, c):
         drain_rows(2 * PART, side_came(step, c))
         if c not in SWAPPED:
             for slot in range(SLOTS):
-                hop(0, slot, 1, c).start()
+                hop(1, slot, 1, c).start()
+                hop(3, slot, 1, c).start()
 
     def on_hop(step, part, c):
         drain_rows(2 * PART, hop_recv.at[step - 1, part, c])
         for slot in range(SLOTS):
-            if step < 3:
-                hop(step, slot, part, c).start()
+            if step == 1:
+                hop(2, slot, part, c).start()
             if c in SWAPPED:
                 beside(step, slot, c).start()
 
@@ -343,14 +344,14 @@
         if c in SWAPPED:
             drain_rows(2 * PART, trade_recv.at[SWAPPED.index(c), step])
         for part in parts_of(c):
-            if step > 1:
-                drain_rows(2 * PART, sum_recv.at[step - 2, part, c])
+            if step == 3:
+                drain_rows(2 * PART, sum_recv.at[1, part, c])
             for slot in range(SLOTS):
                 rows = step_rows(step, slot, part, c)
                 if c in SWAPPED:
                     sums[c // 2, rows, :] += traded(step, slot, c)[...]
-                if step > 1:
-                    sums[c // 2, rows, :] += landing(step - 1, slot, part, c)[...]
+                if step == 3:
+                    sums[c // 2, rows, :] += landing(2, slot, part, c)[...]
         for part in parts_of(c):
             for slot in range(SLOTS):
                 sum_hop(step, slot, part, c).start()
@@ -359,9 +360,11 @@
         if c in SWAPPED:
             drain_rows(2 * PART, trade_recv.at[SWAPPED.index(c), 0])
         for part in parts_of(c):
+            drain_rows(2 * PART, sum_recv.at[0, part, c])
             drain_rows(2 * PART, sum_recv.at[2, part, c])
             for slot in range(SLOTS):
-                value = sums[c // 2, step_rows(0, slot, part, c), :] + landing(3, slot, part, c)[...]
+                value = sums[c // 2, step_rows(0, slot, part, c), :] + landing(1, slot, part, c)[...]
+                value += landing(3, slot, part, c)[...]
                 if part:
                     side_send[side_rows(slot, c), :] = value
                     continue
@@ -479,6 +482,7 @@
     lax.fori_loop(0, CALLS, one_call, 0)
 
     give = remote(total.at[pl.ds(OWN, OWN)], other, own_sem.at[0], own_sem.at[1], twin)
+    pl.semaphore_wait(clear_sem, 1)
     give.start()
     play(OPENING[4])
     give.wait()
@@ -557,6 +561,7 @@
             dma((CHUNKS,)),
             dma((CHUNKS,)),
             dma((len(SWAPPED), 4)),
+            pltpu.SemaphoreType.REGULAR,
         ] + [chunk] * (2 * CHUNKS),
         compiler_params=pltpu.CompilerParams(
             collective_id=0, has_side_effects=True, vmem_limit_bytes=66_000_000),

time: 149 us -> 145 us (0.973)
  Pallas kernels: 149 us -> 145 us
    pallas_call x1, Pallas kernels: 142 us -> 139 us  [run_main(): pl.pallas_call(main_kernel, out_shape=(jax.ShapeDtypeStruct((OWN, WIDTH,...]
where the time goes in v6:
time: 145 us
  Pallas kernels  145 us (100%)
    pallas_call x1, Pallas kernels, run_main(): pl.pallas_call(main_kernel, out_shape=(jax.ShapeDtypeStruct((OWN, WIDTH,...  139 us
    pallas_call x1, Pallas kernels, join(): pl.pallas_call(join_kernel, out_shape=jax.ShapeDtypeStruct((OWN, WIDTH, A...  6.45 us

profile of v6, /device:TPU:0, one launch (start us, length us, event | category | flops | bytes accessed | tf_op | source)
XLA Modules:
  0.0 145.1 jit_solution(5112233655485039860)
XLA Ops:
  0.0 138.6 %main.1 = (f32[12,64,1536]{2,1,0:T(8,128)}, f32[8,64,1536]{2,1,0:T(8,128)}, s32[2,8]{1,0:T(2,128)}) custom-call(s32[1,2]{1,0:T(1,128)} %lists_ref.1, s32[12]{0:T(128)} %orbitals_ref.1, f32[96]{0:T(128)} %occ_ref.1, f32[1,64]{1,0:T(1,128)} %bitcast.1, f32[12,64,1536]{2,1,0:T(8,128)} %held_ref.1), custom_call_target="tpu_custom_call" | custom-call | tf_op jit(solution)/shard_map/main/pallas_call | solution.py:516
  138.6 6.4 %join.1 = f32[12,64,1536]{2,1,0:T(8,128)} custom-call(s32[2,8]{1,0:T(2,128)} %get-tuple-element.8.flags, f32[12,64,1536]{2,1,0:T(8,128)} %get-tuple-element.9.own_ref, f32[8,64,1536]{2,1,0:T(8,128)} %get-tuple-element.10.arrived_ref), custom_call_target="tpu_custom_call" | custom-call | tf_op jit(solution)/shard_map/join/pallas_call | solution.py:582

commit v7 on v6

--- a/solution.py
+++ b/solution.py
@@ -89,11 +89,11 @@
 
 def main_kernel(
     lists_ref, orbitals_ref, occ_ref, vir_ref, held_ref,
-    own_out, arrived, flags,
+    other,
     ints_mine, ints_all, vir_mine, vir_all, ints,
     high, low, total, stack, travel, amp, sums, landed,
-    side_send, side_land, home, other, row_part, column_part,
-    near_land, near_back, swapped,
+    side_send, side_land, home, row_part, column_part,
+    near_land, near_back, swapped, came, flags,
     note_sem, sent_sem, local_sem, swap_sem, box_sem, fetch_recv, side_recv, side_more,
     hop_recv, sum_recv, cross_recv, out_recv, own_sem, near_recv, far_recv, trade_recv, clear_sem,
     *chunks,
@@ -295,12 +295,8 @@
         return remote(home.at[c], near_back.at[c], sent_sem.at[1], far_recv.at[c], facing)
 
     def ship(step, c, x):
-        return remote(box[c].at[pl.ds(step * 2, 2)], arrived.at[pl.ds(x * 2, 2), pl.ds(c * PART, PART)],
-                      sent_sem.at[1], out_recv.at[0], {"grp": held_by(step, 0)})
-
-    def stay(c):
-        return pltpu.make_async_copy(
-            box[c].at[pl.ds(0, 2)], arrived.at[pl.ds(column * 2, 2), pl.ds(c * PART, PART)], local_sem.at[2 + c])
+        return remote(box[c].at[pl.ds(step * 2, 2)], came.at[c, pl.ds(x * 2, 2)],
+                      sent_sem.at[1], out_recv.at[c], {"grp": held_by(step, 0)})
 
     def on_fetch(c):
         drain_rows(6 * PART, fetch_recv.at[c])
@@ -390,14 +386,33 @@
             picks = [jnp.where(row // OWN == held_by(step, 0), one, none) for row in rows]
             return picks[0] * source[c, 0] + picks[1] * source[c, 1]
 
+        def place(step, turn, values):
+            if step:
+                box[c][step * 2 + turn] = values
+            else:
+                came[c, column * 2 + turn] = values
+
         for step in range(4):
-            box[c][step * 2] = blend(mine, home, step)
-        pass_back(c).wait_recv()
+            place(step, 0, blend(mine, home, step))
+        drain_rows(2 * PART, far_recv.at[c])
         for step in range(4):
-            box[c][step * 2 + 1] = blend(theirs, near_back, step)
+            place(step, 1, blend(theirs, near_back, step))
         for step in range(1, 4):
             ship(step, c, column).start()
-        stay(c).start()
+
+    def finish(c):
+        drain_rows(6 * PART, out_recv.at[c])
+        rows = pl.ds(c * PART, PART)
+
+        def add(index, carry):
+            value = total[index, rows, :] + other[index, rows, :]
+            for peer in range(GROUPS):
+                here = (flags[0, peer] == index) & (flags[1, peer] > 0)
+                value += jnp.where(here, one, none) * came[c, peer]
+            other[index, rows, :] = value
+            return carry
+
+        lax.fori_loop(0, OWN, add, 0)
 
     act = {"fetch": on_fetch, "pass": on_pass, "side": on_side, "hop": on_hop, "swap": on_swap,
            "sum": on_sum, "home": on_home, "cross": on_cross, "ship": on_ship}
@@ -487,24 +502,17 @@
     play(OPENING[4])
     give.wait()
 
-    def merge(index, carry):
-        total[index] += other[index]
-        return carry
-
-    lax.fori_loop(0, OWN, merge, 0)
-    store = pltpu.make_async_copy(total.at[pl.ds(0, OWN)], own_out, local_sem.at[0])
-    store.start()
+    order = [place for name, place in [event[:2] for event in OPENING[4]] if name == "ship"]
+    order = [c for c in range(CHUNKS) if c not in order] + order
+    for c in order:
+        finish(c)
     swaps = len(SWAPPED)
     ring_rows = 2 * 3 * SLOTS * PART * (2 * CHUNKS - swaps)
     other_rows = SLOTS * PART * (CHUNKS + 7 * swaps + (CHUNKS - swaps) + CHUNKS + 3 * CHUNKS)
-    for c in range(CHUNKS):
-        stay(c).wait()
     drain(few, note_sem.at[0])
     drain(most, note_sem.at[2])
     drain_rows(ring_rows, sent_sem.at[0])
     drain_rows(other_rows, sent_sem.at[1])
-    drain_rows(3 * SLOTS * WIDTH, out_recv.at[0])
-    store.wait()
 
 
 def run_main(lists, orbitals, occ, vir, held):
@@ -515,13 +523,9 @@
     chunk = pltpu.VMEM((GROUPS, PART, AUX), F32)
     return pl.pallas_call(
         main_kernel,
-        out_shape=(
-            jax.ShapeDtypeStruct((OWN, WIDTH, AUX), F32),
-            jax.ShapeDtypeStruct((GROUPS, WIDTH, AUX), F32),
-            jax.ShapeDtypeStruct((2, GROUPS), jnp.int32),
-        ),
+        out_shape=pltpu.VMEM((OWN, WIDTH, AUX), F32),
         in_specs=[smem, smem, smem, vmem, hbm],
-        out_specs=(hbm, hbm, smem),
+        out_specs=vmem,
         scratch_shapes=[
             pltpu.VMEM((1, LANES), jnp.int32),
             pltpu.VMEM((GROUPS, 1, LANES), jnp.int32),
@@ -539,15 +543,16 @@
             pltpu.VMEM((SLOTS * WIDTH, AUX), F32),
             pltpu.VMEM((SLOTS * WIDTH, AUX), F32),
             pltpu.VMEM((CHUNKS, SLOTS, PART, AUX), F32),
-            pltpu.VMEM((OWN, WIDTH, AUX), F32),
             pltpu.VMEM((ALL, 1), F32),
             pltpu.VMEM((4, 1, STACK), F32),
             pltpu.VMEM((CHUNKS, SLOTS, PART, AUX), F32),
             pltpu.VMEM((CHUNKS, SLOTS, PART, AUX), F32),
             pltpu.VMEM((len(SWAPPED), 4, SLOTS, PART, AUX), F32),
+            pltpu.VMEM((CHUNKS, GROUPS, PART, AUX), F32),
+            pltpu.SMEM((2, GROUPS), jnp.int32),
             dma((4,)),
             dma((2,)),
-            dma((2 + CHUNKS,)),
+            dma((2,)),
             dma((2,)),
             dma((CHUNKS,)),
             dma((CHUNKS,)),
@@ -556,7 +561,7 @@
             dma((3, 2, CHUNKS)),
             dma((3, 2, CHUNKS)),
             dma((CHUNKS,)),
-            dma((1,)),
+            dma((CHUNKS,)),
             dma((2,)),
             dma((CHUNKS,)),
             dma((CHUNKS,)),
@@ -564,41 +569,13 @@
             pltpu.SemaphoreType.REGULAR,
         ] + [chunk] * (2 * CHUNKS),
         compiler_params=pltpu.CompilerParams(
-            collective_id=0, has_side_effects=True, vmem_limit_bytes=66_000_000),
+            collective_id=0, has_side_effects=True, vmem_limit_bytes=62_000_000),
         name="main",
     )(lists, orbitals, occ, vir, held)
 
 
-def join_kernel(flags, own_ref, arrived_ref, out_ref):
-    out_ref[...] = own_ref[...]
-    for peer in range(GROUPS):
-        @pl.when(flags[1, peer] > 0)
-        def _():
-            out_ref[flags[0, peer]] += arrived_ref[peer]
-
-
-def join(flags, own, arrived):
-    height = 16
-    return pl.pallas_call(
-        join_kernel,
-        out_shape=jax.ShapeDtypeStruct((OWN, WIDTH, AUX), F32),
-        grid_spec=pltpu.PrefetchScalarGridSpec(
-            num_scalar_prefetch=1,
-            grid=(WIDTH // height,),
-            in_specs=[
-                pl.BlockSpec((OWN, height, AUX), lambda i, *_: (0, i, 0)),
-                pl.BlockSpec((GROUPS, height, AUX), lambda i, *_: (0, i, 0)),
-            ],
-            out_specs=pl.BlockSpec((OWN, height, AUX), lambda i, *_: (0, i, 0)),
-        ),
-        name="join",
-    )(flags, own, arrived)
-
-
 def body(integrals, pair_lists, row_orbital, occ_energy, vir_energy):
-    own, arrived, flags = run_main(
-        pair_lists, row_orbital, occ_energy, vir_energy.reshape(1, WIDTH), integrals)
-    return join(flags, own, arrived)
+    return run_main(pair_lists, row_orbital, occ_energy, vir_energy.reshape(1, WIDTH), integrals)
 
 
 def solution(mesh):

time: 145 us -> 141 us (0.972)
  Pallas kernels: 145 us -> 138 us
  local copies, waits for them, and re-layouts: 0 us -> 2.19 us
    pallas_call x2 -> x1, Pallas kernels: 145 us -> 138 us  [run_main(): pl.pallas_call(main_kernel, out_shape=pltpu.VMEM((OWN, WIDTH, AUX), F32),...]
    unnamed x0 -> x1, local copies, waits for them, and re-layouts: none -> 2.19 us
where the time goes in v7:
time: 141 us
  Pallas kernels  138 us (98%)
  local copies, waits for them, and re-layouts  2.19 us (2%)
    pallas_call x1, Pallas kernels, run_main(): pl.pallas_call(main_kernel, out_shape=pltpu.VMEM((OWN, WIDTH, AUX), F32),...  138 us

profile of v7, /device:TPU:0, one launch (start us, length us, event | category | flops | bytes accessed | tf_op | source)
XLA Modules:
  0.0 140.6 jit_solution(35623575039200522)
XLA Ops:
  0.0 138.4 %main.1 = f32[12,64,1536]{2,1,0:T(8,128)S(1)} custom-call(s32[1,2]{1,0:T(1,128)} %lists_ref.1, s32[12]{0:T(128)} %orbitals_ref.1, f32[96]{0:T(128)} %occ_ref.1, f32[1,64]{1,0:T(1,128)} %bitcast.1, f32[12,64,1536]{2,1,0:T(8,128)} %held_ref.1), custom_call_target="tpu_custom_call" | custom-call | tf_op jit(solution)/shard_map/main/pallas_call | solution.py:524
  138.4 2.2 %copy.7 = f32[12,64,1536]{2,1,0:T(8,128)} copy(f32[12,64,1536]{2,1,0:T(8,128)S(1)} %main.1) | data formatting | bytes 9437184

commit v8 on v7

--- a/solution.py
+++ b/solution.py
@@ -17,8 +17,10 @@
 HELD = OWN * WIDTH
 ALL = 2 * HELD
 CHUNKS = 8
-SWAPPED = (2, 5)
+SWAPPED = (3, 5)
 HEAD = 8
+STRAIGHT_IN = (0, 1)
+STRAIGHT_OUT = (7,)
 PART = WIDTH // CHUNKS
 CALLS = 4
 PIECE = WIDTH // CALLS
@@ -30,51 +32,48 @@
 NT = (((1,), (1,)), ((), ()))
 TN = (((0,), (0,)), ((), ()))
 OPENING = {
-    0: [("fetch", 0), ("fetch", 1), ("pass", 0), ("hop", 1, 0, 0), ("fetch", 2), ("hop", 3, 0, 0), ("pass", 1),
-        ("side", 0, 0), ("hop", 2, 0, 0), ("hop", 1, 0, 1), ("fetch", 3), ("pass", 2), ("hop", 3, 0, 1),
-        ("hop", 1, 1, 0), ("side", 0, 1), ("hop", 3, 1, 0), ("hop", 2, 0, 1), ("fetch", 4), ("pass", 3),
-        ("hop", 3, 0, 2), ("side", 0, 2), ("hop", 2, 1, 0), ("hop", 1, 0, 2), ("hop", 1, 1, 1), ("fetch", 5),
-        ("hop", 3, 1, 1), ("pass", 4), ("hop", 3, 0, 3), ("side", 0, 3), ("hop", 2, 0, 2), ("side", 3, 2),
-        ("fetch", 6), ("hop", 2, 1, 1)],
-    4: [("sum", 3, 6), ("ship", 1), ("cross", 4), ("sum", 1, 7), ("home", 5), ("ship", 3), ("sum", 3, 7),
-        ("ship", 4), ("home", 6), ("ship", 5), ("cross", 6), ("home", 7), ("ship", 6), ("cross", 7), ("ship", 7)],
+    0: [("fetch", 0), ("hop", 1, 0, 0), ("side", 0, 0), ("fetch", 1), ("hop", 3, 0, 0), ("fetch", 2),
+        ("hop", 2, 0, 0), ("side", 0, 1), ("hop", 1, 1, 0), ("hop", 3, 1, 0), ("hop", 1, 0, 1), ("fetch", 3),
+        ("hop", 3, 0, 1), ("pass", 2), ("hop", 1, 1, 1), ("hop", 3, 1, 1), ("hop", 2, 1, 0), ("fetch", 4),
+        ("hop", 2, 0, 1), ("pass", 3), ("hop", 1, 0, 2), ("side", 0, 2), ("hop", 3, 0, 2), ("hop", 2, 1, 1)],
+    1: [("hop", 3, 1, 4), ("pass", 6), ("side", 0, 5), ("sum", 3, 0), ("side", 2, 3)],
+    4: [("ship", 2), ("cross", 4), ("sum", 3, 6), ("sum", 3, 7), ("ship", 5), ("ship", 4), ("home", 6),
+        ("home", 7), ("cross", 6), ("cross", 7), ("ship", 7), ("ship", 6)],
 }
 BETWEEN = {
-    (0, 0, 0): [("side", 1, 2), ("hop", 1, 0, 3), ("hop", 1, 0, 4), ("hop", 3, 0, 4)],
-    (0, 0, 1): [("fetch", 7), ("hop", 1, 1, 3)],
-    (0, 0, 2): [("pass", 5), ("hop", 2, 0, 3), ("hop", 3, 1, 3), ("side", 0, 4)],
-    (0, 1, 0): [("hop", 2, 0, 4)],
-    (0, 1, 1): [("side", 2, 2), ("hop", 2, 1, 3), ("hop", 1, 0, 5)],
-    (0, 1, 2): [("hop", 3, 0, 5), ("sum", 2, 0), ("sum", 1, 0)],
-    (0, 2, 0): [("hop", 1, 1, 4), ("hop", 3, 1, 4)],
-    (0, 2, 1): [("hop", 2, 0, 5), ("sum", 2, 1)],
-    (0, 2, 2): [("side", 0, 5)],
-    (1, 0, 0): [("pass", 6), ("side", 1, 5)],
-    (1, 0, 1): [("pass", 7), ("hop", 2, 1, 4), ("side", 3, 5)],
-    (1, 0, 2): [("side", 2, 5), ("sum", 3, 0)],
-    (1, 1, 0): [("hop", 1, 0, 6)],
-    (1, 1, 1): [("side", 0, 6), ("hop", 3, 0, 6), ("hop", 1, 0, 7)],
-    (1, 1, 2): [("side", 0, 7), ("hop", 3, 0, 7), ("swap", 0, 2), ("swap", 1, 2), ("swap", 2, 2), ("swap", 3, 2)],
-    (1, 2, 0): [("home", 0)],
-    (1, 2, 1): [("hop", 2, 0, 6), ("sum", 3, 1)],
-    (1, 2, 2): [("hop", 1, 1, 6), ("hop", 3, 1, 6)],
-    (2, 0, 0): [("hop", 1, 1, 7), ("hop", 2, 0, 7)],
-    (2, 0, 1): [("hop", 3, 1, 7), ("sum", 1, 1)],
-    (2, 0, 2): [("sum", 2, 2), ("sum", 1, 2)],
-    (2, 1, 0): [("hop", 2, 1, 6), ("sum", 2, 3)],
-    (2, 1, 1): [("hop", 2, 1, 7), ("cross", 0)],
-    (2, 1, 2): [("swap", 0, 5), ("swap", 1, 5), ("swap", 2, 5), ("swap", 3, 5), ("home", 1), ("sum", 1, 3)],
-    (2, 2, 0): [("sum", 3, 2)],
-    (2, 2, 1): [("sum", 2, 4)],
-    (2, 2, 2): [("ship", 0), ("sum", 3, 3)],
-    (3, 0, 0): [("home", 2), ("sum", 1, 4)],
-    (3, 0, 1): [("sum", 1, 5)],
-    (3, 0, 2): [("sum", 3, 4)],
-    (3, 1, 0): [("home", 3), ("sum", 2, 5)],
-    (3, 1, 1): [("cross", 1)],
-    (3, 1, 2): [("sum", 2, 6), ("sum", 1, 6)],
-    (3, 2, 0): [("ship", 2), ("home", 4)],
-    (3, 2, 1): [("cross", 3), ("sum", 3, 5), ("sum", 2, 7)],
+    (0, 0, 0): [("fetch", 5), ("pass", 4), ("hop", 1, 0, 3)],
+    (0, 0, 1): [("hop", 2, 0, 2), ("side", 0, 3), ("hop", 3, 0, 3)],
+    (0, 0, 2): [("fetch", 6), ("hop", 1, 1, 2)],
+    (0, 1, 0): [("hop", 3, 1, 2), ("hop", 1, 0, 4)],
+    (0, 1, 1): [("pass", 5), ("hop", 2, 0, 3), ("side", 0, 4), ("hop", 3, 0, 4)],
+    (0, 1, 2): [("fetch", 7), ("hop", 2, 1, 2), ("side", 1, 3), ("sum", 2, 0)],
+    (0, 2, 0): [("hop", 2, 0, 4), ("sum", 1, 0)],
+    (0, 2, 1): [("side", 3, 3), ("hop", 1, 0, 5), ("hop", 3, 0, 5)],
+    (0, 2, 2): [("hop", 1, 1, 4)],
+    (1, 0, 0): [("sum", 2, 1)],
+    (1, 0, 1): [("pass", 7), ("hop", 2, 1, 4), ("hop", 2, 0, 5)],
+    (1, 0, 2): [("side", 1, 5), ("hop", 1, 0, 6), ("hop", 3, 0, 6)],
+    (1, 1, 0): [("side", 3, 5), ("sum", 1, 1)],
+    (1, 1, 1): [("side", 0, 6), ("home", 0)],
+    (1, 1, 2): [("swap", 0, 3), ("swap", 1, 3), ("swap", 2, 3), ("side", 0, 7), ("hop", 1, 0, 7), ("swap", 3, 3)],
+    (1, 2, 0): [("hop", 3, 0, 7)],
+    (1, 2, 1): [("side", 2, 5), ("hop", 2, 0, 6)],
+    (1, 2, 2): [("cross", 0), ("sum", 3, 1)],
+    (2, 0, 0): [("hop", 1, 1, 6), ("hop", 3, 1, 6), ("sum", 2, 2)],
+    (2, 0, 1): [("hop", 1, 1, 7), ("hop", 3, 1, 7)],
+    (2, 0, 2): [("hop", 2, 0, 7), ("sum", 1, 2)],
+    (2, 1, 0): [("home", 1)],
+    (2, 1, 1): [("hop", 2, 1, 6), ("sum", 2, 3), ("sum", 1, 3)],
+    (2, 1, 2): [("swap", 0, 5), ("swap", 1, 5), ("swap", 2, 5), ("swap", 3, 5), ("sum", 3, 2)],
+    (2, 2, 0): [("hop", 2, 1, 7), ("ship", 0), ("cross", 1), ("sum", 2, 4)],
+    (2, 2, 2): [("sum", 3, 3), ("sum", 1, 4)],
+    (3, 0, 0): [("home", 2), ("sum", 1, 5)],
+    (3, 0, 1): [("sum", 2, 5)],
+    (3, 0, 2): [("home", 3), ("sum", 3, 4)],
+    (3, 1, 2): [("ship", 1), ("cross", 2), ("sum", 3, 5), ("sum", 2, 6)],
+    (3, 2, 0): [("home", 4), ("sum", 1, 6)],
+    (3, 2, 1): [("ship", 3), ("sum", 2, 7)],
+    (3, 2, 2): [("home", 5), ("sum", 1, 7)],
 }
 
 
@@ -192,11 +191,17 @@
         return remote(box[c].at[pl.ds(step * 2, 2)], got[c].at[pl.ds(x * 2, 2)],
                       box_sem.at[c], fetch_recv.at[c], {"grp": held_by(step, 0)})
 
+    def fetch_straight(step, turn, c):
+        return remote(box[c].at[step * 2 + turn], got[c].at[column * 2 + turn],
+                      box_sem.at[c], fetch_recv.at[c], {"grp": held_by(step, turn)})
+
+    others = [(step, turn) for step in range(4) for turn in range(2) if step or turn]
+
     def fill(c):
         for step in range(4):
             for turn in range(2):
                 values = other[flags[0, lax.rem(column + step, 4) * 2 + turn], pl.ds(c * PART, PART), :]
-                if step == 0:
+                if step == 0 and not (turn and c in STRAIGHT_IN):
                     got[c][column * 2 + turn] = values
                 else:
                     box[c][step * 2 + turn] = values
@@ -205,6 +210,10 @@
     for c in range(CHUNKS):
         if c + 1 < CHUNKS:
             fill(c + 1)
+        if c in STRAIGHT_IN:
+            for step, turn in others:
+                fetch_straight(step, turn, c).start()
+            continue
         for step in range(1, 4):
             fetch(step, c, column).start()
 
@@ -299,16 +308,27 @@
                       sent_sem.at[1], out_recv.at[c], {"grp": held_by(step, 0)})
 
     def on_fetch(c):
+        if c in STRAIGHT_IN:
+            drain_rows(7 * PART, fetch_recv.at[c])
+            spread(c)
+            return
         drain_rows(6 * PART, fetch_recv.at[c])
         for slot in range(SLOTS):
             box[c][slot] = got[c][their_columns[slot] * 2 + 1]
         pass_on(c).start()
 
     def on_pass(c):
-        pass_on(c).wait_recv()
+        drain_rows(2 * PART, near_recv.at[c])
+        spread(c)
+
+    def spread(c):
         for slot in range(SLOTS):
-            stack[c // 2, step_rows(0, slot, 0, c), :] = (
-                got[c][columns[slot] * 2] * level_with[slot] + near_land[c, slot] * opposed[slot])
+            near = got[c][columns[slot] * 2] * level_with[slot]
+            if c in STRAIGHT_IN:
+                near += got[c][columns[slot] * 2 + 1] * opposed[slot]
+            else:
+                near += near_land[c, slot] * opposed[slot]
+            stack[c // 2, step_rows(0, slot, 0, c), :] = near
         for slot in range(SLOTS):
             beside(0, slot, c).start()
             hop(1, slot, 0, c).start()
@@ -377,31 +397,43 @@
         drain_rows(2 * PART, cross_recv.at[c])
         for slot in range(SLOTS):
             home[c, slot] += side_land[side_rows(slot, c), :]
-        pass_back(c).start()
+        if c not in STRAIGHT_OUT:
+            pass_back(c).start()
+
+    def ship_straight(step, turn, c):
+        return remote(box[c].at[step * 2 + turn], came.at[c, column * 2 + turn],
+                      sent_sem.at[2], out_recv.at[c], {"grp": held_by(step, turn)})
 
     def on_ship(c):
-        drain_rows(8 * PART, box_sem.at[c])
-
-        def blend(rows, source, step):
-            picks = [jnp.where(row // OWN == held_by(step, 0), one, none) for row in rows]
+        drain_rows((7 if c in STRAIGHT_IN else 8) * PART, box_sem.at[c])
+
+        def blend(rows, source, step, turn):
+            picks = [jnp.where(row // OWN == held_by(step, turn), one, none) for row in rows]
             return picks[0] * source[c, 0] + picks[1] * source[c, 1]
 
         def place(step, turn, values):
-            if step:
+            if step or (turn and c in STRAIGHT_OUT):
                 box[c][step * 2 + turn] = values
             else:
                 came[c, column * 2 + turn] = values
 
+        if c in STRAIGHT_OUT:
+            for step in range(4):
+                for turn in range(2):
+                    place(step, turn, blend(mine, home, step, turn))
+            for step, turn in others:
+                ship_straight(step, turn, c).start()
+            return
         for step in range(4):
-            place(step, 0, blend(mine, home, step))
+            place(step, 0, blend(mine, home, step, 0))
         drain_rows(2 * PART, far_recv.at[c])
         for step in range(4):
-            place(step, 1, blend(theirs, near_back, step))
+            place(step, 1, blend(theirs, near_back, step, 0))
         for step in range(1, 4):
             ship(step, c, column).start()
 
     def finish(c):
-        drain_rows(6 * PART, out_recv.at[c])
+        drain_rows((7 if c in STRAIGHT_OUT else 6) * PART, out_recv.at[c])
         rows = pl.ds(c * PART, PART)
 
         def add(index, carry):
@@ -508,11 +540,13 @@
         finish(c)
     swaps = len(SWAPPED)
     ring_rows = 2 * 3 * SLOTS * PART * (2 * CHUNKS - swaps)
-    other_rows = SLOTS * PART * (CHUNKS + 7 * swaps + (CHUNKS - swaps) + CHUNKS + 3 * CHUNKS)
+    other_rows = SLOTS * PART * (
+        CHUNKS + 7 * swaps + (CHUNKS - swaps) + 4 * (CHUNKS - len(STRAIGHT_OUT)))
     drain(few, note_sem.at[0])
     drain(most, note_sem.at[2])
     drain_rows(ring_rows, sent_sem.at[0])
     drain_rows(other_rows, sent_sem.at[1])
+    drain(total.at[pl.ds(0, 7 * len(STRAIGHT_OUT)), pl.ds(0, PART)], sent_sem.at[2])
 
 
 def run_main(lists, orbitals, occ, vir, held):
@@ -551,7 +585,7 @@
             pltpu.VMEM((CHUNKS, GROUPS, PART, AUX), F32),
             pltpu.SMEM((2, GROUPS), jnp.int32),
             dma((4,)),
-            dma((2,)),
+            dma((3,)),
             dma((2,)),
             dma((2,)),
             dma((CHUNKS,)),

time: 141 us -> 134 us (0.950)
  Pallas kernels: 138 us -> 132 us
    pallas_call x1, Pallas kernels: 138 us -> 132 us  [run_main(): pl.pallas_call(main_kernel, out_shape=pltpu.VMEM((OWN, WIDTH, AUX), F32),...]
where the time goes in v8:
time: 134 us
  Pallas kernels  132 us (99%)
  local copies, waits for them, and re-layouts  2.19 us (2%)
    pallas_call x1, Pallas kernels, run_main(): pl.pallas_call(main_kernel, out_shape=pltpu.VMEM((OWN, WIDTH, AUX), F32),...  132 us

profile of v8, /device:TPU:0, one launch (start us, length us, event | category | flops | bytes accessed | tf_op | source)
XLA Modules:
  0.0 134.1 jit_solution(84445336845262652)
XLA Ops:
  0.0 131.9 %main.1 = f32[12,64,1536]{2,1,0:T(8,128)S(1)} custom-call(s32[1,2]{1,0:T(1,128)} %lists_ref.1, s32[12]{0:T(128)} %orbitals_ref.1, f32[96]{0:T(128)} %occ_ref.1, f32[1,64]{1,0:T(1,128)} %bitcast.1, f32[12,64,1536]{2,1,0:T(8,128)} %held_ref.1), custom_call_target="tpu_custom_call" | custom-call | tf_op jit(solution)/shard_map/main/pallas_call | solution.py:558
  131.9 2.2 %copy.7 = f32[12,64,1536]{2,1,0:T(8,128)} copy(f32[12,64,1536]{2,1,0:T(8,128)S(1)} %main.1) | data formatting | bytes 9437184

commit v9 on v8

--- a/solution.py
+++ b/solution.py
@@ -37,8 +37,8 @@
         ("hop", 3, 0, 1), ("pass", 2), ("hop", 1, 1, 1), ("hop", 3, 1, 1), ("hop", 2, 1, 0), ("fetch", 4),
         ("hop", 2, 0, 1), ("pass", 3), ("hop", 1, 0, 2), ("side", 0, 2), ("hop", 3, 0, 2), ("hop", 2, 1, 1)],
     1: [("hop", 3, 1, 4), ("pass", 6), ("side", 0, 5), ("sum", 3, 0), ("side", 2, 3)],
-    4: [("ship", 2), ("cross", 4), ("sum", 3, 6), ("sum", 3, 7), ("ship", 5), ("ship", 4), ("home", 6),
-        ("home", 7), ("cross", 6), ("cross", 7), ("ship", 7), ("ship", 6)],
+    4: [("ship", 2), ("cross", 4), ("sum", 3, 6), ("sum", 3, 7), ("ship", 5), ("home", 6), ("home", 7),
+        ("ship", 4), ("cross", 6), ("cross", 7), ("ship", 7), ("ship", 6)],
 }
 BETWEEN = {
     (0, 0, 0): [("fetch", 5), ("pass", 4), ("hop", 1, 0, 3)],

time: 134 us -> 134 us (level)
  no operation moved by 1% of the time
where the time goes in v9:
time: 134 us
  Pallas kernels  132 us (99%)
  local copies, waits for them, and re-layouts  2.19 us (2%)
    pallas_call x1, Pallas kernels, run_main(): pl.pallas_call(main_kernel, out_shape=pltpu.VMEM((OWN, WIDTH, AUX), F32),...  132 us

profile of v9, /device:TPU:0, one launch (start us, length us, event | category | flops | bytes accessed | tf_op | source)
XLA Modules:
  0.0 134.1 jit_solution(15576877238008114518)
XLA Ops:
  0.0 131.9 %main.1 = f32[12,64,1536]{2,1,0:T(8,128)S(1)} custom-call(s32[1,2]{1,0:T(1,128)} %lists_ref.1, s32[12]{0:T(128)} %orbitals_ref.1, f32[96]{0:T(128)} %occ_ref.1, f32[1,64]{1,0:T(1,128)} %bitcast.1, f32[12,64,1536]{2,1,0:T(8,128)} %held_ref.1), custom_call_target="tpu_custom_call" | custom-call | tf_op jit(solution)/shard_map/main/pallas_call | solution.py:558
  131.9 2.2 %copy.7 = f32[12,64,1536]{2,1,0:T(8,128)} copy(f32[12,64,1536]{2,1,0:T(8,128)S(1)} %main.1) | data formatting | bytes 9437184
